TPU v7x, 256 devices: a whole 4x4x8 slice. The times are simulated.
256 devices in a mesh: seq: 64 (over z, y, x_lo), tp: 4 (over x_hi, core).
Axes of the slice: x: 4 (x_hi: 2, x_lo: 2; x = x_hi * 2 + x_lo), y: 4, z: 8, core: 2. Of those that a mesh axis runs over, the one named last changes fastest.
Arguments:
- hidden_in: bfloat16 [24576, 3072], P('seq', 'tp'), may hold values from -6 to 6
- norm_gain: bfloat16 [3072], replicated, may hold values from 0.5 to 1.5
- w_query: bfloat16 [3072, 1536], P(None, 'tp')
- w_key: bfloat16 [3072, 512], P(None, 'tp')
- w_value: bfloat16 [3072, 512], P(None, 'tp'), may hold values from -0.109375 to 0.109375
- w_out: bfloat16 [1536, 3072], P('tp'), may hold values from -0.3125 to 0.3125
- short_lengths: int32 [14], replicated, may hold values from 256 to 1024, as said below
- page_slot: int32 [384], replicated, may hold values from 0 to 383, each once
Outputs:
- hidden_out: bfloat16 [24576, 3072], P('seq', 'tp')
- cache_pool: bfloat16 [384, 2, 64, 512], P('seq', None, None, 'tp')
Inputs may be any that keep to these rules, and one draw needn't show every extreme that they name: `short_lengths`: multiples of 64; at least one short prompt has 1024 tokens; together they have 24576 - 16512 tokens. `page_slot`: each slot is named by exactly one page.
All inputs are finite; a program needn't handle non-finite values.
Results may differ from a plain program's by a relative error of at most 0.015.
Values may be sent and summed in bfloat16 or wider, within the bound.
A program may use at most 128 MiB of HBM per device.

v0:
```python
import jax
import jax.numpy as jnp
from jax import lax
from jax.sharding import PartitionSpec as P

QH = 12
KVH = 4
HD = 128
PAGE = 64


rope_base = 500000.0
norm_eps = 1e-05
neg_large = -1e30


def packed_position(row_ids, rows_per_dev, seq_count):
    block_rows = rows_per_dev // 2
    device = row_ids // rows_per_dev
    second = row_ids // block_rows % 2
    block_id = jnp.where(second == 0, device, 2 * seq_count - 1 - device)
    return block_id * block_rows + row_ids % block_rows


def storage_row(positions, rows_per_dev, seq_count):
    block_rows = rows_per_dev // 2
    block_id = positions // block_rows
    device = jnp.where(block_id < seq_count, block_id, 2 * seq_count - 1 - block_id)
    second = jnp.where(block_id < seq_count, 0, 1)
    return device * rows_per_dev + second * block_rows + positions % block_rows


def prompt_start(positions, short_lengths, long_len):
    prompt_ends = long_len + jnp.cumsum(short_lengths)
    bounds = jnp.concatenate(
        [jnp.zeros((1,), jnp.int32), jnp.reshape(long_len, (1,)), prompt_ends[:-1]]
    )
    at_or_before = bounds[None, :] <= positions[:, None]
    return jnp.max(jnp.where(at_or_before, bounds[None, :], 0), axis=1)


def rotate(values, relative, head_size):
    half_size = head_size // 2
    frequency = rope_base ** (-(jnp.arange(half_size, dtype=jnp.float32) * 2.0) / head_size)
    angles = relative.astype(jnp.float32)[:, None] * frequency[None, :]
    cosine = jnp.concatenate([jnp.cos(angles), jnp.cos(angles)], axis=1)[:, None, :]
    sine_part = jnp.concatenate([jnp.sin(angles), jnp.sin(angles)], axis=1)[:, None, :]
    turned = jnp.concatenate([-values[..., half_size:], values[..., :half_size]], axis=-1)
    return values * cosine + turned * sine_part


def project(row_data, norm_gain, w_query, w_key, w_value, relative, head_size):
    wide = row_data.astype(jnp.float32)
    squares = jnp.mean(wide * wide, axis=1, keepdims=True)
    normed = (wide * lax.rsqrt(squares + norm_eps) * norm_gain.astype(jnp.float32)[None, :]).astype(
        jnp.bfloat16
    )
    row_count = row_data.shape[0]
    query_rows = jnp.dot(normed, w_query, preferred_element_type=jnp.float32).reshape(
        row_count, -1, head_size
    )
    key_rows = jnp.dot(normed, w_key, preferred_element_type=jnp.float32).reshape(
        row_count, -1, head_size
    )
    value_rows = jnp.dot(normed, w_value, preferred_element_type=jnp.float32).astype(jnp.bfloat16)
    query_rows = rotate(query_rows, relative, head_size).astype(jnp.bfloat16).reshape(row_count, -1)
    key_rows = rotate(key_rows, relative, head_size).astype(jnp.bfloat16).reshape(row_count, -1)
    return (query_rows, key_rows, value_rows)


def attend_block(carried, query_blk, key_blk, value_blk, allowed_pairs, group_size, head_size):
    running_max, denominator, accumulated = carried
    row_count = query_blk.shape[0]
    key_count = key_blk.shape[0]
    queries = query_blk.reshape(row_count, -1, group_size, head_size)
    keys_local = key_blk.reshape(key_count, -1, head_size)
    values_local = value_blk.reshape(key_count, -1, head_size)
    scores = jnp.einsum(
        "rkgd,skd->rkgs", queries, keys_local, preferred_element_type=jnp.float32
    ) * (1.0 / jnp.sqrt(jnp.float32(head_size)))
    visible = allowed_pairs[:, None, None, :]
    scores = jnp.where(visible, scores, neg_large)
    new_max = jnp.maximum(running_max, jnp.max(scores, axis=-1))
    weights = jnp.where(visible, jnp.exp(scores - new_max[..., None]), 0.0)
    factor = jnp.exp(running_max - new_max)
    denominator = denominator * factor + jnp.sum(weights, axis=-1)
    accumulated = accumulated * factor[..., None] + jnp.einsum(
        "rkgs,skd->rkgd",
        weights.astype(jnp.bfloat16),
        values_local,
        preferred_element_type=jnp.float32,
    )
    return (new_max, denominator, accumulated)


def local(hidden_in, norm_gain, w_query, w_key, w_value, w_out, short_lengths, page_slot):
    seq_count = lax.axis_size("seq")
    seq_index = lax.axis_index("seq")
    rows_per_dev = hidden_in.shape[0]
    block_rows = rows_per_dev // 2
    head_size = HD
    group_size = QH // KVH
    total_rows = rows_per_dev * seq_count
    long_len = total_rows - jnp.sum(short_lengths)
    gathered = lax.all_gather(hidden_in, "tp", axis=1, tiled=True)
    row_ids = seq_index * rows_per_dev + jnp.arange(rows_per_dev, dtype=jnp.int32)
    positions = packed_position(row_ids, rows_per_dev, seq_count)
    prompt_first = prompt_start(positions, short_lengths, long_len)
    query_rows, key_rows, value_rows = project(
        gathered, norm_gain, w_query, w_key, w_value, positions - prompt_first, head_size
    )
    kv_heads = key_rows.shape[1] // head_size
    key_width = key_rows.shape[1]
    pages_dev = rows_per_dev // PAGE
    slot_ids = seq_index * pages_dev + jnp.arange(pages_dev, dtype=jnp.int32)
    page_ids = jnp.arange(page_slot.shape[0], dtype=jnp.int32)
    wanted = jnp.sum(
        jnp.where(page_slot[None, :] == slot_ids[:, None], page_ids[None, :], 0), axis=1
    )
    wanted_pos = wanted[:, None] * PAGE + jnp.arange(PAGE, dtype=jnp.int32)[None, :]
    wanted_rows = storage_row(wanted_pos, rows_per_dev, seq_count)

    def empty_state():
        return (
            jnp.full((block_rows, kv_heads, group_size), neg_large, jnp.float32),
            jnp.zeros((block_rows, kv_heads, group_size), jnp.float32),
            jnp.zeros((block_rows, kv_heads, group_size, head_size), jnp.float32),
        )

    half_states = (empty_state(), empty_state())
    page_pool = jnp.zeros((pages_dev, 2, PAGE, key_width), jnp.bfloat16)
    key_piece = lax.all_gather(key_rows, "seq", axis=0, tiled=True)
    value_piece = lax.all_gather(value_rows, "seq", axis=0, tiled=True)
    row_count = key_piece.shape[0]
    sub_rows = min(row_count, block_rows)
    sub_count = row_count // sub_rows
    new_states = []
    for fold_half_index in range(2):
        query_blk = query_rows[fold_half_index * block_rows : (fold_half_index + 1) * block_rows]
        query_pos = positions[fold_half_index * block_rows : (fold_half_index + 1) * block_rows]
        query_first = prompt_first[
            fold_half_index * block_rows : (fold_half_index + 1) * block_rows
        ]

        def over_keys(step_index, state_now):
            local_first = step_index * sub_rows
            key_blk = lax.dynamic_slice_in_dim(key_piece, local_first, sub_rows, 0)
            value_blk = lax.dynamic_slice_in_dim(value_piece, local_first, sub_rows, 0)
            key_pos = packed_position(
                local_first + jnp.arange(sub_rows, dtype=jnp.int32), rows_per_dev, seq_count
            )
            allowed_pairs = (key_pos[None, :] >= query_first[:, None]) & (
                key_pos[None, :] <= query_pos[:, None]
            )

            def attend_now(state_in):
                return attend_block(
                    state_in, query_blk, key_blk, value_blk, allowed_pairs, group_size, head_size
                )

            def keep_state(state_in):
                return state_in

            return lax.cond(jnp.any(allowed_pairs), attend_now, keep_state, state_now)

        new_states.append(lax.fori_loop(0, sub_count, over_keys, half_states[fold_half_index]))
    inside = (wanted_rows >= 0) & (wanted_rows < row_count)
    picked = jnp.clip(wanted_rows, 0, row_count - 1).reshape(-1)
    taken_keys = jnp.take(key_piece, picked, axis=0).reshape(pages_dev, PAGE, key_width)
    taken_values = jnp.take(value_piece, picked, axis=0).reshape(pages_dev, PAGE, key_width)
    taken = jnp.stack([taken_keys, taken_values], axis=1)
    page_pool = jnp.where(inside[:, None, :, None], taken, page_pool)
    final_states, page_pool = ((new_states[0], new_states[1]), page_pool)
    attended_parts = []
    for half_index in range(2):
        running_max, denominator, accumulated = final_states[half_index]
        attended_parts.append(
            (accumulated / denominator[..., None]).astype(jnp.bfloat16).reshape(block_rows, -1)
        )
    attended = jnp.concatenate(attended_parts, axis=0)
    column_count = hidden_in.shape[1]
    partial_terms = jnp.dot(attended, w_out, preferred_element_type=jnp.float32)
    summed = lax.psum(partial_terms.astype(jnp.bfloat16), "tp").astype(jnp.float32)
    own_share = lax.dynamic_slice_in_dim(
        summed, lax.axis_index("tp") * column_count, column_count, 1
    )
    hidden_out = (hidden_in.astype(jnp.float32) + own_share).astype(jnp.bfloat16)
    return (hidden_out, page_pool)


def solution(mesh):
    placed = (
        P("seq", "tp"),
        P(),
        P(None, "tp"),
        P(None, "tp"),
        P(None, "tp"),
        P("tp", None),
        P(),
        P(),
    )
    return jax.shard_map(
        local,
        mesh=mesh,
        in_specs=placed,
        out_specs=(P("seq", "tp"), P("seq", None, None, "tp")),
        check_vma=False,
    )
```

profile of v0, /device:TPU:193, one launch (start us, length us, event | category | flops | bytes accessed | tf_op | source)
XLA Modules:
  0.0 1437.1 jit_solution(391605902127887108)
XLA Ops:
  12.1 29.6 %all-gather.4.cloned.1.call-done = bf16[384,3072]{1,0:T(8,128)(2,1)} async-done(((bf16[384,768]{1,0:T(8,128)(2,1)}), bf16[384,3072]{1,0:T(8,128)(2,1)}) %all-gather.4.cloned.1.call-update) | async-done | bytes 2359312 | tf_op jit(solution)/shard_map/all_gather | solution.py:105
  43.9 2.8 fusion.83
  47.5 3.3 convolution_convert_fusion.1
  51.4 4.7 fusion.81
  58.9 233.9 %all-gather.6.cloned.1.call-done = bf16[24576,128]{0,1:T(8,128)(2,1)} async-done(((bf16[384,128]{0,1:T(8,128)(2,1)}), bf16[24576,128]{0,1:T(8,128)(2,1)}) %all-gather.6.cloned.1.call-update) | async-done | bytes 6291472 | tf_op jit(solution)/shard_map/all_gather | solution.py:132
  292.8 8.6 copy.46
  301.4 298.8 %all-gather.8.cloned.1.call-done = bf16[24576,128]{1,0:T(8,128)(2,1)} async-done(((bf16[384,128]{1,0:T(8,128)(2,1)}), bf16[24576,128]{1,0:T(8,128)(2,1)}) %all-gather.8.cloned.1.call-update) | async-done | bytes 6291472 | tf_op jit(solution)/shard_map/all_gather | solution.py:133
  600.3 309.8 %while.40 = (s32[]{:T(128)}, f32[192,1,3]{0,2,1:T(4,128)S(1)}, f32[192,1,3]{0,2,1:T(4,128)S(1)}, f32[192,1,3,128]{3,0,2,1:T(8,128)S(1)}, s32[192]{0:T(256)S(1)},...) while((s32[]{:T(128)}, f32[192,1,3]{0,2,1:T(4,128)S(1)}, ...), condition=%wide.region_10.11_spmd, body=%wide.region_4.10_spmd.sunk | while | flops 57921800 | bytes 2350373 | solution.py:166
  607.1 2.5 conditional.4
  612.6 2.5 conditional.4
  618.0 2.5 conditional.4
  655.9 2.5 conditional.4
  661.4 2.5 conditional.4
  666.8 2.5 conditional.4
  672.2 2.5 conditional.4
  710.2 2.5 conditional.4
  715.6 2.5 conditional.4
  721.0 2.5 conditional.4
  759.0 2.5 conditional.4
  764.4 2.5 conditional.4
  769.8 2.5 conditional.4
  775.3 2.5 conditional.4
  813.2 2.5 conditional.4
  818.6 2.5 conditional.4
  824.1 2.5 conditional.4
  862.0 2.5 conditional.4
  910.5 386.7 %while.41 = (s32[]{:T(128)}, f32[192,1,3]{0,2,1:T(4,128)S(1)}, f32[192,1,3]{0,2,1:T(4,128)S(1)}, f32[192,1,3,128]{3,0,2,1:T(8,128)S(1)}, s32[192]{0:T(256)S(1)},...) while((s32[]{:T(128)}, f32[192,1,3]{0,2,1:T(4,128)S(1)}, ...), condition=%wide.region_17.18_spmd, body=%wide.region_11.17_spmd.sunk | while | flops 57921800 | bytes 2350373 | solution.py:166
  949.9 2.5 conditional.5
  1297.5 2.8 convolution_convert_fusion
  1301.0 4.8 gather_fusion
  1305.8 4.8 gather_fusion.1
  1311.5 117.1 %all-reduce.2.cloned.1.call-done = bf16[384,3072]{1,0:T(8,128)(2,1)} async-done(((bf16[384,3072]{1,0:T(8,128)(2,1)}), bf16[384,3072]{1,0:T(8,128)(2,1)}) %all-reduce.2.cloned.1.call-update) | async-done | bytes 2359312 | tf_op jit(solution)/shard_map/psum | solution.py:183
  (1586 shorter events, 806.9 us)
Async XLA Ops:
  7.2 1290.3 %copy-start = (bf16[384,3072]{1,0:T(8,128)(2,1)S(1)}, bf16[384,3072]{1,0:T(8,128)(2,1)}, u32[]{:S(2)}) copy-start(bf16[384,3072]{1,0:T(8,128)(2,1)} %param.23) | copy-start | bytes 7077892
  7.2 34.5 %all-gather.4.cloned.1.call-start = ((), (), s32[]{:S(2)}) async-start(), calls=%async_computation | async-start | bytes 2949120 | tf_op jit(solution)/shard_map/all_gather | solution.py:105
  7.9 284.8 %all-gather.6.cloned.1.call-start = ((), (), s32[]{:S(2)}) async-start(), calls=%async_computation.1 | async-start | bytes 6389760 | tf_op jit(solution)/shard_map/all_gather | solution.py:132
  47.5 552.7 %all-gather.8.cloned.1.call-start = ((), (), s32[]{:S(2)}) async-start(), calls=%async_computation.2 | async-start | bytes 6389760 | tf_op jit(solution)/shard_map/all_gather | solution.py:133
  50.8 1377.7 %all-reduce.2.cloned.1.call-start = ((), (), s32[]{:S(2)}) async-start(), calls=%async_computation.3 | async-start | bytes 4718592 | tf_op jit(solution)/shard_map/psum | solution.py:183
  1297.2 3.2 copy-start.2
  1297.5 131.0 %copy-start.1 = (bf16[384,768]{1,0:T(8,128)(2,1)S(1)}, bf16[384,768]{1,0:T(8,128)(2,1)}, u32[]{:S(2)}) copy-start(bf16[384,768]{1,0:T(8,128)(2,1)} %param.18) | copy-start | bytes 1769476
Sparse Core Ops, SparseCore 0:
  9.8 31.8 all-gather.3
  47.6 245.1 all-gather.5
  294.6 305.6 all-gather.7
  1300.5 128.0 all-reduce.1
where the time goes:
time: 1460 us; the launch traced here: 1440 us
  waiting for transfers between devices  680 us (47%)
  matrix products  309 us (21%)
  other arithmetic  231 us (16%)
  loops' own time  181 us (12%)
  local copies, waits for them, and re-layouts  21 us (1%)
  between operations  14.7 us (1%)
    all_gather x1, waiting for transfers between devices, local(): value_piece = lax.all_gather(value_rows, 'seq', axis=0, tiled=True)  299 us
    all_gather x1, waiting for transfers between devices, local(): key_piece = lax.all_gather(key_rows, 'seq', axis=0, tiled=True)  234 us
    and x256, other arithmetic, over_keys(): (key_pos[None, :] >= query_first[:, None]) & (key_pos[None, :] <= query_p...  192 us
    another operation x2, loops' own time, local(): lax.fori_loop(0, sub_count, over_keys, half_states[fold_half_index])  174 us
    dot_general x129, matrix products, attend_block(): jnp.einsum('rkgs,skd->rkgd', weights.astype(jnp.bfloat16), values_local,...  154 us
    dot_general x129, matrix products, attend_block(): jnp.einsum('rkgd,skd->rkgs', queries, keys_local, preferred_element_type=...  141 us
    psum x1, waiting for transfers between devices, local(): lax.psum(partial_terms.astype(jnp.bfloat16), 'tp').astype(jnp.float32)  117 us
    all_gather x1, waiting for transfers between devices, local(): gathered = lax.all_gather(hidden_in, 'tp', axis=1, tiled=True)  29.6 us
  transfers between devices with their start and end apart: 4, of which 4 were waited for; matrix products, arithmetic and copies ran while one was open for 2% of the time, Pallas kernels for 0%

commit v1 on v0

v1 whole, which is shorter than its diff:
```python
import functools
import heapq
import math

import jax
import jax.numpy as jnp
from jax import lax
from jax.experimental import pallas as pl
from jax.experimental.pallas import tpu as pltpu
from jax.sharding import PartitionSpec as P

MESH = pl.DeviceIdType.MESH
F32 = jnp.float32
BF16 = jnp.bfloat16

D = 3072
QH = 12
KVH = 4
HD = 128
PAGE = 64
GROUP = 3
N_SEQ = 64
N_TP = 4
ROWS = 384
BLOCK = 192
COLS = D // N_TP
HEAD_COLS = GROUP * HD
LONG = 16512
LONG_BLOCKS = LONG // BLOCK
THIRD = 64
rope_base = 500000.0
norm_eps = 1e-05
SCALE2 = math.log2(math.e) / math.sqrt(HD)
NEG = -1e30


def onward(color, off, via):
    dz, dy, dx = off
    order = ("xyz", "xzy", "zyx")[color]
    if via == "own":
        links = []
        for axis in order:
            links += ["x"] if axis == "x" else [axis + "+", axis + "-"]
        return links
    links = []
    if via == "z+" and (dz in (-1, -2) or (dz == -3 and (color == 2 or dx == 0))):
        links.append(via)
    if via == "z-" and (dz in (1, 2) or (dz == 3 and color != 2 and dx == 1)):
        links.append(via)
    if via == "y+" and dy == -1 and (dz % 2 == 0 if color == 2 else dx == 0):
        links.append(via)
    if via == "y-" and dy == 1 and (dz % 2 == 1 if color == 2 else dx == 1):
        links.append(via)
    for axis in order[order.index(via[0]) + 1 :]:
        links += ["x"] if axis == "x" else [axis + "+", axis + "-"]
    return links


def shifted(off, link):
    dz, dy, dx = off
    dz += {"z+": -1, "z-": 1}.get(link, 0)
    dy += {"y+": -1, "y-": 1}.get(link, 0)
    dx ^= int(link == "x")
    return (4 if dz == -4 else dz, 2 if dy == -2 else dy, dx)


def arrival_order(copy_us=1.41, hop_us=1.7):
    free, heap, events, count = {}, [], [], 0

    def issue(now, color, off, links):
        nonlocal count
        for link in links:
            first = max(now, free.get(link, 0.0))
            free[link] = first + copy_us
            count += 1
            heapq.heappush(
                heap, (first + copy_us + hop_us, count, color, shifted(off, link), link)
            )

    for color in range(3):
        issue(0.0, color, (0, 0, 0), onward(color, (0, 0, 0), "own"))
    while heap:
        now, _, color, off, link = heapq.heappop(heap)
        links = onward(color, off, link)
        events.append((color, off, links))
        issue(now, color, off, links)
    return events


EVENTS = arrival_order()
OFFSETS = sorted({off for _, off, _ in EVENTS})


def places():
    seq = lax.axis_index("seq")
    tp = lax.axis_index("tp")
    return seq // 8, (seq // 2) % 4, seq % 2, tp // 2, tp % 2


def seq_of(z, y, x_lo):
    return z * 8 + y * 2 + x_lo


def x_neighbours():
    z, y, x_lo, x_hi, core = places()
    x = x_hi * 2 + x_lo
    ids = []
    for step in (1, 3):
        other = lax.rem(x + step, 4)
        ids.append((seq_of(z, y, other % 2), (other // 2) * 2 + core))
    return x, ids


def greet(ids):
    barrier = pltpu.get_barrier_semaphore()
    for one in ids:
        pl.semaphore_signal(barrier, inc=1, device_id=one, device_id_type=MESH)
    pl.semaphore_wait(barrier, len(ids))


def remote(src, dst, send, recv, target):
    return pltpu.make_async_remote_copy(
        src_ref=src, dst_ref=dst, send_sem=send, recv_sem=recv, device_id=target,
        device_id_type=MESH,
    )


CHUNKS = 3
CHUNK = BLOCK // CHUNKS


def project_kernel(
    hidden, gain, wq, wk, wv, cosine, sine, q_out, kv_out,
    xbuf, relay, wbuf, wsem, own_sem, send_sem, r0, r1, r2, r3,
):
    z, y, x_lo, x_hi, core = places()
    seq = lax.axis_index("seq")
    tp = lax.axis_index("tp")
    loads = [
        pltpu.make_async_copy(wq, wbuf.at[:, 0:HEAD_COLS], wsem.at[0]),
        pltpu.make_async_copy(wk, wbuf.at[:, HEAD_COLS : HEAD_COLS + HD], wsem.at[1]),
        pltpu.make_async_copy(wv, wbuf.at[:, HEAD_COLS + HD : HEAD_COLS + 2 * HD], wsem.at[2]),
        pltpu.make_async_copy(hidden, xbuf.at[tp], own_sem),
    ]
    for one in loads:
        one.start()
    x, sides = x_neighbours()
    partner = (seq, x_hi * 2 + 1 - core)
    greet([partner] + sides)
    sends = []

    def go(copy):
        copy.start()
        sends.append(copy)
        return copy

    firsts = {}
    for c in range(CHUNKS):
        for way in range(2):
            rows = pl.ds(way * BLOCK + c * CHUNK, CHUNK)
            k = way * CHUNKS + c
            firsts[k] = go(
                remote(hidden.at[rows], relay.at[k], send_sem.at[k], r1.at[k], sides[way])
            )
    own = go(remote(hidden, xbuf.at[tp], send_sem.at[18], r0, partner))
    opposite = (1 - x_hi) * 2 + core
    seconds = {}

    def pass_on(k):
        way, c = k // CHUNKS, k % CHUNKS
        firsts[k].wait_recv()
        source = lax.rem(x + (3 if way == 0 else 1), 4)
        rows = pl.ds(way * BLOCK + c * CHUNK, CHUNK)
        seconds[k] = go(
            remote(
                relay.at[k], xbuf.at[(source // 2) * 2 + core, rows], send_sem.at[6 + k], r2.at[k],
                sides[way],
            )
        )

    thirds = {}

    def share(k):
        way, c = k // CHUNKS, k % CHUNKS
        rows = pl.ds(way * BLOCK + c * CHUNK, CHUNK)
        remote(
            relay.at[k], xbuf.at[opposite, rows], send_sem.at[6 + k], r2.at[k], sides[way]
        ).wait_recv()
        thirds[k] = go(
            remote(
                xbuf.at[opposite, rows], xbuf.at[opposite, rows], send_sem.at[12 + k], r3.at[k],
                partner,
            )
        )

    for c in range(CHUNKS):
        for way in range(2):
            pass_on(way * CHUNKS + c)
        if c >= 1:
            for way in range(2):
                share(way * CHUNKS + c - 1)
    for way in range(2):
        share(way * CHUNKS + CHUNKS - 1)
    for one in loads:
        one.wait()
    own.wait_recv()
    for k in range(2 * CHUNKS):
        thirds[k].wait_recv()
    for one in sends:
        one.wait_send()
    squares = jnp.zeros((ROWS, 1), F32)
    for part in range(N_TP):
        wide = xbuf[part].astype(F32)
        squares += jnp.sum(wide * wide, axis=1, keepdims=True)
    factor = lax.rsqrt(squares * (1.0 / D) + norm_eps)
    total = jnp.zeros((ROWS, HEAD_COLS + 2 * HD), F32)
    for part in range(N_TP):
        cols = slice(part * COLS, (part + 1) * COLS)
        normed = (xbuf[part].astype(F32) * factor * gain[:, cols].astype(F32)).astype(BF16)
        total += jnp.dot(normed, wbuf[cols, :], preferred_element_type=F32)
    cos = cosine[...]
    sin = sine[...]
    for head in range(GROUP + 1):
        u = total[:, head * HD : (head + 1) * HD]
        turned = (u * cos + pltpu.roll(u, HD // 2, 1) * sin).astype(BF16)
        for half in range(2):
            rows = slice(half * BLOCK, (half + 1) * BLOCK)
            if head < GROUP:
                q_out[half, head] = turned[rows]
            else:
                kv_out[half] = turned[rows].reshape(BLOCK // THIRD, THIRD, HD)
    value = total[:, HEAD_COLS + HD :].astype(BF16)
    for half in range(2):
        kv_out[2 + half] = value[half * BLOCK : (half + 1) * BLOCK].reshape(
            BLOCK // THIRD, THIRD, HD
        )


TILE_SLOTS = 4
TILE = TILE_SLOTS * BLOCK
N_TILES = N_SEQ // TILE_SLOTS


def attend_kernel(
    wanted, q, kv, first_b, attended, pages, buf, m_ref, l_ref, acc_ref, own_sem, send_sem, recv_sem
):
    z, y, x_lo, x_hi, core = places()
    seq = lax.axis_index("seq")
    tp = lax.axis_index("tp")
    own = pltpu.make_async_copy(kv, buf.at[:, seq], own_sem)
    own.start()
    target = {
        "x": (seq_of(z, y, 1 - x_lo), tp),
        "y+": (seq_of(z, lax.rem(y + 1, 4), x_lo), tp),
        "y-": (seq_of(z, lax.rem(y + 3, 4), x_lo), tp),
        "z+": (seq_of(lax.rem(z + 1, 8), y, x_lo), tp),
        "z-": (seq_of(lax.rem(z + 7, 8), y, x_lo), tp),
    }
    greet(list(target.values()))

    def chunk(color, off):
        dz, dy, dx = off
        slot = seq_of(
            lax.rem(z + (dz + 8), 8), lax.rem(y + (dy + 4), 4), x_lo if dx == 0 else 1 - x_lo
        )
        return buf.at[:, slot, color]

    def send(color, off, link, src):
        there = shifted(off, link)
        remote(
            src, chunk(color, off), send_sem.at[color],
            recv_sem.at[color, OFFSETS.index(there)], target[link],
        ).start()

    for color in range(3):
        for link in onward(color, (0, 0, 0), "own"):
            send(color, (0, 0, 0), link, kv.at[:, color])
    for color, off, links in EVENTS:
        here = chunk(color, off)
        remote(
            here, here, send_sem.at[color], recv_sem.at[color, OFFSETS.index(off)], target["x"]
        ).wait_recv()
        for link in links:
            send(color, off, link, here)
    own.wait()
    for color in range(3):
        sent = buf.at[:, pl.ds(0, N_SEQ - 1), color]
        pltpu.make_async_copy(sent, sent, send_sem.at[color]).wait()

    m_ref[...] = jnp.full(m_ref.shape, NEG, F32)
    l_ref[...] = jnp.zeros(l_ref.shape, F32)
    acc_ref[...] = jnp.zeros(acc_ref.shape, F32)

    def step(half, region, tile, allowed):
        rows = pl.ds(tile * TILE_SLOTS, TILE_SLOTS)
        keys = buf[region, rows].reshape(TILE, HD)
        values = buf[2 + region, rows].reshape(TILE, HD)
        for head in range(GROUP):
            scores = lax.dot_general(
                q[half, head], keys, (((1,), (1,)), ((), ())), preferred_element_type=F32
            )
            if allowed is not None:
                scores = jnp.where(allowed, scores, NEG)
            old = m_ref[half, head]
            new = jnp.maximum(old, jnp.max(scores, axis=1, keepdims=True))
            weights = jnp.exp2(scores * SCALE2 - new * SCALE2)
            if allowed is not None:
                weights = jnp.where(allowed, weights, 0.0)
            keep = jnp.exp2((old - new) * SCALE2)
            m_ref[half, head] = new
            l_ref[half, head] = l_ref[half, head] * keep + jnp.sum(weights, axis=1, keepdims=True)
            acc_ref[half, head] = acc_ref[half, head] * keep + jnp.dot(
                weights.astype(BF16), values, preferred_element_type=F32
            )

    row = lax.broadcasted_iota(jnp.int32, (BLOCK, TILE), 0)
    col = lax.broadcasted_iota(jnp.int32, (BLOCK, TILE), 1)
    slot_in = (
        (col >= BLOCK).astype(jnp.int32)
        + (col >= 2 * BLOCK).astype(jnp.int32)
        + (col >= 3 * BLOCK).astype(jnp.int32)
    )
    back = col - 2 * BLOCK * slot_in
    own_tile = seq // TILE_SLOTS
    last_block = 2 * N_SEQ - 1
    step(0, 0, own_tile, col + own_tile * TILE <= row + seq * BLOCK)

    @pl.loop(0, own_tile)
    def _(tile):
        step(0, 0, tile, None)

    row_pos = row + (last_block - seq) * BLOCK

    def masked_b(tile):
        key_pos = back + (last_block - tile * TILE_SLOTS) * BLOCK
        step(1, 1, tile, (key_pos <= row_pos) & (key_pos >= first_b[...]))

    masked_b(own_tile)
    in_long = (seq + (LONG_BLOCKS - N_SEQ)) // N_SEQ
    short_tiles = (seq + 6) // TILE_SLOTS - own_tile

    @pl.loop(own_tile + 1, own_tile + 1 + (1 - in_long) * short_tiles)
    def _(tile):
        masked_b(tile)

    @pl.loop(N_TILES - in_long * (N_TILES - 1 - own_tile), N_TILES)
    def _(tile):
        step(1, 1, tile, None)

    @pl.loop(0, in_long * N_TILES)
    def _(tile):
        step(1, 0, tile, None)

    for half in range(2):
        for head in range(GROUP):
            attended[half * BLOCK : (half + 1) * BLOCK, head * HD : (head + 1) * HD] = (
                acc_ref[half, head] / l_ref[half, head]
            ).astype(BF16)
    for page in range(ROWS // PAGE):
        region = wanted[page, 0]
        slot = wanted[page, 1]
        part = wanted[page, 2]
        pages[page, 0] = buf[region, slot, part]
        pages[page, 1] = buf[region + 2, slot, part]


def output_kernel(
    attended, w_out, hidden, out, sendp, recvp, sendx, recvx, relay, send_sem, rp, r1, r2
):
    z, y, x_lo, x_hi, core = places()
    seq = lax.axis_index("seq")
    x, sides = x_neighbours()
    partner = (seq, x_hi * 2 + 1 - core)
    greet([partner] + sides)

    def terms(part):
        cols = pl.ds(pl.multiple_of(part * COLS, COLS), COLS)
        return jnp.dot(attended[...], w_out[:, cols], preferred_element_type=F32)

    sends = []

    def go(copy):
        copy.start()
        sends.append(copy)
        return copy

    far = (1 - x_hi) * 2
    near = x_hi * 2
    sendp[0] = terms(far + 1 - core).astype(BF16)
    far_copy = go(remote(sendp.at[0], recvp.at[0], send_sem.at[12], rp.at[0], partner))
    mine = terms(far + core)
    far_copy.wait_recv()
    sendx[...] = (mine + recvp[0].astype(F32)).astype(BF16)
    firsts = {}
    for c in range(CHUNKS):
        for way in range(2):
            rows = pl.ds(way * BLOCK + c * CHUNK, CHUNK)
            k = way * CHUNKS + c
            firsts[k] = go(
                remote(sendx.at[rows], relay.at[k], send_sem.at[k], r1.at[k], sides[way])
            )
    sendp[1] = terms(near + 1 - core).astype(BF16)
    near_copy = go(remote(sendp.at[1], recvp.at[1], send_sem.at[13], rp.at[1], partner))
    seconds = {}
    for c in range(CHUNKS):
        for way in range(2):
            k = way * CHUNKS + c
            rows = pl.ds(way * BLOCK + c * CHUNK, CHUNK)
            firsts[k].wait_recv()
            seconds[k] = go(
                remote(relay.at[k], recvx.at[rows], send_sem.at[6 + k], r2.at[k], sides[way])
            )
    kept = terms(near + core) + hidden[...].astype(F32)
    near_copy.wait_recv()
    kept = kept + recvp[1].astype(F32)
    for k in range(2 * CHUNKS):
        seconds[k].wait_recv()
    out[...] = (kept + recvx[...].astype(F32)).astype(BF16)
    for one in sends:
        one.wait_send()


VM = pl.BlockSpec(memory_space=pltpu.VMEM)
ANY = pl.BlockSpec(memory_space=pl.ANY)
DMA = pltpu.SemaphoreType.DMA


def params(cid, mib):
    return pltpu.CompilerParams(
        collective_id=cid, has_side_effects=True, vmem_limit_bytes=mib * 1024 * 1024
    )


def row_facts(short_lengths, page_slot):
    seq = lax.axis_index("seq")
    rows = jnp.arange(ROWS, dtype=jnp.int32)
    offset = rows % BLOCK
    block = jnp.where(rows < BLOCK, seq, 2 * N_SEQ - 1 - seq)
    positions = block * BLOCK + offset
    ends = LONG + jnp.cumsum(short_lengths)
    bounds = jnp.concatenate([jnp.full((1,), LONG, jnp.int32), ends[:-1]])
    first = jnp.max(
        jnp.where(bounds[None, :] <= positions[:, None], bounds[None, :], 0), axis=1
    )
    relative = (positions - first).astype(F32)
    half = HD // 2
    frequency = rope_base ** (-(jnp.arange(half, dtype=F32) * 2.0) / HD)
    angles = relative[:, None] * frequency[None, :]
    cos = jnp.cos(angles)
    sin = jnp.sin(angles)
    cosine = jnp.concatenate([cos, cos], axis=1)
    sine = jnp.concatenate([-sin, sin], axis=1)
    pages_dev = ROWS // PAGE
    slots = seq * pages_dev + jnp.arange(pages_dev, dtype=jnp.int32)
    ids = jnp.arange(page_slot.shape[0], dtype=jnp.int32)
    page = jnp.sum(jnp.where(page_slot[None, :] == slots[:, None], ids[None, :], 0), axis=1)
    page_block = page // (BLOCK // PAGE)
    late = page_block >= N_SEQ
    wanted = jnp.stack(
        [
            late.astype(jnp.int32),
            jnp.where(late, 2 * N_SEQ - 1 - page_block, page_block),
            page % (BLOCK // PAGE),
        ],
        axis=1,
    )
    return cosine, sine, first[BLOCK:, None], wanted


def local(hidden_in, norm_gain, w_query, w_key, w_value, w_out, short_lengths, page_slot):
    cosine, sine, first_b, wanted = row_facts(short_lengths, page_slot)
    q, kv = pl.pallas_call(
        project_kernel,
        out_shape=(
            jax.ShapeDtypeStruct((2, GROUP, BLOCK, HD), BF16),
            jax.ShapeDtypeStruct((4, BLOCK // THIRD, THIRD, HD), BF16),
        ),
        in_specs=[VM, VM, ANY, ANY, ANY, VM, VM],
        out_specs=(VM, VM),
        scratch_shapes=[
            pltpu.VMEM((N_TP, ROWS, COLS), BF16),
            pltpu.VMEM((2 * CHUNKS, CHUNK, COLS), BF16),
            pltpu.VMEM((D, HEAD_COLS + 2 * HD), BF16),
            DMA((3,)),
            DMA(()),
            DMA((19,)),
            DMA(()),
            DMA((2 * CHUNKS,)),
            DMA((2 * CHUNKS,)),
            DMA((2 * CHUNKS,)),
        ],
        compiler_params=params(0, 40),
        name="gather_project",
    )(hidden_in, norm_gain.reshape(1, D), w_query, w_key, w_value, cosine, sine)
    attended, pages = pl.pallas_call(
        attend_kernel,
        out_shape=(
            jax.ShapeDtypeStruct((ROWS, HEAD_COLS), BF16),
            jax.ShapeDtypeStruct((ROWS // PAGE, 2, PAGE, HD), BF16),
        ),
        in_specs=[pl.BlockSpec(memory_space=pltpu.SMEM), VM, VM, VM],
        out_specs=(VM, VM),
        scratch_shapes=[
            pltpu.VMEM((4, N_SEQ, BLOCK // THIRD, THIRD, HD), BF16),
            pltpu.VMEM((2, GROUP, BLOCK, 1), F32),
            pltpu.VMEM((2, GROUP, BLOCK, 1), F32),
            pltpu.VMEM((2, GROUP, BLOCK, HD), F32),
            DMA(()),
            DMA((3,)),
            DMA((3, len(OFFSETS))),
        ],
        compiler_params=params(1, 60),
        name="gather_attend",
    )(wanted, q, kv, first_b)
    hidden_out = pl.pallas_call(
        output_kernel,
        out_shape=jax.ShapeDtypeStruct((ROWS, COLS), BF16),
        in_specs=[VM, VM, VM],
        out_specs=VM,
        scratch_shapes=[
            pltpu.VMEM((2, ROWS, COLS), BF16),
            pltpu.VMEM((2, ROWS, COLS), BF16),
            pltpu.VMEM((ROWS, COLS), BF16),
            pltpu.VMEM((ROWS, COLS), BF16),
            pltpu.VMEM((2 * CHUNKS, CHUNK, COLS), BF16),
            DMA((14,)),
            DMA((2,)),
            DMA((2 * CHUNKS,)),
            DMA((2 * CHUNKS,)),
        ],
        compiler_params=params(2, 40),
        name="project_reduce",
    )(attended, w_out, hidden_in)
    return hidden_out, pages


def solution(mesh):
    placed = (
        P("seq", "tp"),
        P(),
        P(None, "tp"),
        P(None, "tp"),
        P(None, "tp"),
        P("tp", None),
        P(),
        P(),
    )
    return jax.shard_map(
        local,
        mesh=mesh,
        in_specs=placed,
        out_specs=(P("seq", "tp"), P("seq", None, None, "tp")),
        check_vma=False,
    )
```

time: 1460 us -> 178 us (0.12); the launches traced: 1440 us -> 178 us
  waiting for transfers between devices: 680 us -> 0 us
  matrix products: 309 us -> 0 us
  other arithmetic: 231 us -> 3.55 us
  loops' own time: 181 us -> 0 us
  Pallas kernels: 0 us -> 163 us
    all_gather x3 -> x0, waiting for transfers between devices: 562 us -> none  [the longest x1 299 us: local(): value_piece = lax.all_gather(value_rows, 'seq', axis=0, tiled=True)]
    dot_general x262 -> x0, matrix products: 309 us -> none  [the longest x129 154 us: attend_block(): jnp.einsum('rkgs,skd->rkgd', weights.astype(jnp.bfloat16), values_local,...]
    and x258 -> x0, other arithmetic: 192 us -> none  [the longest x256 192 us: over_keys(): (key_pos[None, :] >= query_first[:, None]) & (key_pos[None, :] <= query_p...]
    another operation x258 -> x0, loops' own time: 181 us -> none  [the longest x2 174 us: local(): lax.fori_loop(0, sub_count, over_keys, half_states[fold_half_index])]
    pallas_call x0 -> x3, Pallas kernels: none -> 163 us  [the longest x1 118 us: local(): pl.pallas_call(attend_kernel, out_shape=(jax.ShapeDtypeStruct((ROWS, HEAD...]
    psum x1 -> x0, waiting for transfers between devices: 117 us -> none  [local(): lax.psum(partial_terms.astype(jnp.bfloat16), 'tp').astype(jnp.float32)]
    reduce_sum x132 -> x1, other arithmetic: 21.9 us -> 0.87 us  [row_facts(): jnp.sum(jnp.where(page_slot[None, :] == slots[:, None], ids[None, :], 0),...]
  transfers between devices with their start and end apart: 4 -> 0, of which waited for: 4 -> 0; matrix products, arithmetic and copies ran while one was open for 2% -> 0% of each run, Pallas kernels for 0% -> 0%
where the time goes in v1:
time: 178 us
  Pallas kernels  163 us (92%)
  local copies, waits for them, and re-layouts  10.7 us (6%)
  other arithmetic  3.55 us (2%)
    pallas_call x1, Pallas kernels, local(): pl.pallas_call(attend_kernel, out_shape=(jax.ShapeDtypeStruct((ROWS, HEAD...  118 us
    pallas_call x1, Pallas kernels, local(): pl.pallas_call(project_kernel, out_shape=(jax.ShapeDtypeStruct((2, GROUP,...  23.8 us
    pallas_call x1, Pallas kernels, local(): pl.pallas_call(output_kernel, out_shape=jax.ShapeDtypeStruct((ROWS, COLS)...  20.5 us
    unnamed x22, local copies, waits for them, and re-layouts  8.83 us

profile of v1, /device:TPU:193, one launch (start us, length us, event | category | flops | bytes accessed | tf_op | source)
XLA Modules:
  0.0 177.5 jit_solution(9996143956229917214)
XLA Ops:
  0.6 0.9 select_reduce_fusion.1
  1.5 0.8 reduce-window.9
  2.4 0.1 pad_add_fusion.1
  2.4 0.1 copy.26
  2.6 0.1 select_reduce_fusion
  2.7 0.1 slice.11
  2.8 0.1 copy.27
  2.9 0.1 copy.25
  3.0 0.7 pad_add_fusion.wanted
  3.6 0.7 reshape.134.gain
  4.3 0.8 copy.32.first_b
  5.1 0.8 fusion
  5.9 0.2 pad_maximum_fusion
  6.1 0.0 copy-start
  6.1 1.7 copy-done
  7.7 0.0 copy-start.2
  7.7 1.1 copy-done.2
  8.8 1.1 copy-done.4
  9.9 1.1 copy-done.5
  11.1 23.8 %gather_project.1 = (bf16[2,3,192,128]{3,2,1,0:T(8,128)(2,1)S(1)}, bf16[4,3,64,128]{3,2,1,0:T(8,128)(2,1)S(1)}) custom-call(bf16[384,768]{1,0:T(8,128)(2,1)S(1)} %copy-done.2, bf16[1,3072]{1,0:T(2,128)(2,1)S(1)} %reshape.134.gain, bf16[3072,384]{1,0:T(8,128)(2,1)S(1)} %copy-done, bf16[3072,128]{1,0:T(8,128)(2,1)S(1)} %copy-done.4, ...), custom_call_target="tpu_custom_call" | custom-call | tf_op jit(solution)/shard_map/gather_project/pallas_call | solution.py:472
  34.9 0.0 copy-start.6
  34.9 0.7 copy-done.6
  35.6 0.7 copy-done.8
  36.3 118.3 %gather_attend.1 = (bf16[384,384]{1,0:T(8,128)(2,1)}, bf16[6,2,64,128]{3,2,1,0:T(8,128)(2,1)}) custom-call(s32[6,3]{1,0:T(8,128)} %pad_add_fusion.wanted, bf16[2,3,192,128]{3,2,1,0:T(8,128)(2,1)} %copy-done.6, bf16[4,3,64,128]{3,2,1,0:T(8,128)(2,1)} %copy-done.8, s32[192,1]{1,0:T(8,128)} %copy.32.first_b), custom_call_target="tpu_custom_call" | custom-call | tf_op jit(solution)/shard_map/gather_attend/pallas_call | solution.py:495
  154.5 0.0 copy-done.1
  154.5 0.0 copy-done.3
  154.6 0.0 copy-start.7
  154.6 1.0 copy-done.7
  155.5 20.5 %project_reduce.1 = bf16[384,768]{1,0:T(8,128)(2,1)S(1)} custom-call(bf16[384,384]{1,0:T(8,128)(2,1)S(1)} %copy-done.7, bf16[384,3072]{1,0:T(8,128)(2,1)S(1)} %copy-done.1, bf16[384,768]{1,0:T(8,128)(2,1)S(1)} %copy-done.3), custom_call_target="tpu_custom_call" | custom-call | tf_op jit(solution)/shard_map/project_reduce/pallas_call | solution.py:515
  176.0 0.8 copy.35
  176.8 0.0 copy-done.9
  176.8 0.7 copy.36
  (16 shorter events, 0.1 us)
Async XLA Ops:
  6.1 1.7 copy-start
  7.7 1.1 copy-start.2
  8.8 1.1 copy-start.4
  9.9 1.1 copy-start.5
  11.1 143.5 %copy-start.1 = (bf16[384,3072]{1,0:T(8,128)(2,1)S(1)}, bf16[384,3072]{1,0:T(8,128)(2,1)}, u32[]{:S(2)}) copy-start(bf16[384,3072]{1,0:T(8,128)(2,1)} %w_out.1) | copy-start | bytes 7077892
  11.1 143.5 %copy-start.3 = (bf16[384,768]{1,0:T(8,128)(2,1)S(1)}, bf16[384,768]{1,0:T(8,128)(2,1)}, u32[]{:S(2)}) copy-start(bf16[384,768]{1,0:T(8,128)(2,1)} %hidden.3) | copy-start | bytes 1769476
  34.9 0.7 copy-start.6
  35.6 0.7 copy-start.8
  154.6 1.0 copy-start.7
  155.5 21.3 %copy-start.9 = (bf16[6,2,64,128]{3,2,1,0:T(8,128)(2,1)S(1)}, bf16[6,2,64,128]{3,2,1,0:T(8,128)(2,1)}, u32[]{:S(2)}) copy-start(bf16[6,2,64,128]{3,2,1,0:T(8,128)(2,1)} %get-tuple-element.22) | copy-start | bytes 589828

commit v2 on v1

v2 whole, which is shorter than its diff:
```python
import functools
import heapq
import math

import jax
import jax.numpy as jnp
import numpy as np
from jax import lax
from jax.experimental import pallas as pl
from jax.experimental.pallas import tpu as pltpu
from jax.sharding import PartitionSpec as P

MESH = pl.DeviceIdType.MESH
F32 = jnp.float32
BF16 = jnp.bfloat16

D = 3072
QH = 12
KVH = 4
HD = 128
PAGE = 64
GROUP = 3
N_SEQ = 64
N_TP = 4
ROWS = 384
BLOCK = 192
COLS = D // N_TP
HEAD_COLS = GROUP * HD
LONG = 16512
LONG_BLOCKS = LONG // BLOCK
THIRD = 64
rope_base = 500000.0
norm_eps = 1e-05
SCALE2 = math.log2(math.e) / math.sqrt(HD)
NEG = -1e30


def onward(color, off, via):
    dz, dy, dx = off
    order = ("xyz", "xzy", "zyx")[color]
    if via == "own":
        links = []
        for axis in order:
            links += ["x"] if axis == "x" else [axis + "+", axis + "-"]
        return links
    links = []
    if via == "z+" and (dz in (-1, -2) or (dz == -3 and (color == 2 or dx == 0))):
        links.append(via)
    if via == "z-" and (dz in (1, 2) or (dz == 3 and color != 2 and dx == 1)):
        links.append(via)
    if via == "y+" and dy == -1 and (dz % 2 == 0 if color == 2 else dx == 0):
        links.append(via)
    if via == "y-" and dy == 1 and (dz % 2 == 1 if color == 2 else dx == 1):
        links.append(via)
    for axis in order[order.index(via[0]) + 1 :]:
        links += ["x"] if axis == "x" else [axis + "+", axis + "-"]
    return links


def shifted(off, link):
    dz, dy, dx = off
    dz += {"z+": -1, "z-": 1}.get(link, 0)
    dy += {"y+": -1, "y-": 1}.get(link, 0)
    dx ^= int(link == "x")
    return (4 if dz == -4 else dz, 2 if dy == -2 else dy, dx)


def plan(copy_us=1.41, hop_us=1.7, step_us=1.0, first_us=1.5):
    free, heap, count, now = {}, [], 0, 0.0

    def issue(color, off, links):
        nonlocal count
        for link in links:
            first = max(now, free.get(link, 0.0))
            free[link] = first + copy_us
            count += 1
            heapq.heappush(
                heap, (first + copy_us + hop_us, count, color, shifted(off, link), link)
            )

    for color in range(3):
        issue(color, (0, 0, 0), onward(color, (0, 0, 0), "own"))
    now = first_us
    missing = [set() for _ in range(STEPS // 3)]
    for unit in range(STEPS // 3):
        dz = plane_of(unit // 2)
        for dy in (0, 1, -1, 2) if unit % 2 else (0, 1, -1):
            for dx in (0, 1):
                missing[unit] |= {(color, (dz, dy, dx)) for color in range(3)}
        missing[unit] -= {(color, (0, 0, 0)) for color in range(3)}
    taken, batches, batch, step = set(), [], [], 0
    while step < STEPS or heap:
        if heap and heap[0][0] <= now:
            _, _, color, off, link = heapq.heappop(heap)
            links = onward(color, off, link)
            taken.add((color, off))
            batch.append((color, off, links))
            now += 0.03
            issue(color, off, links)
        elif step < STEPS and missing[step // 3] <= taken:
            batches.append(batch)
            batch = []
            step += 1
            now += step_us
        else:
            now = heap[0][0]
    return batches, now


N_TILES = 16
STEPS = 3 * N_TILES


def plane_of(rank):
    return (rank + 1) // 2 * (1 - 2 * ((rank + 1) % 2))


BATCHES, _ = plan()
OFFSETS = sorted({off for batch in BATCHES for _, off, _ in batch})


def places():
    seq = lax.axis_index("seq")
    tp = lax.axis_index("tp")
    return seq // 8, (seq // 2) % 4, seq % 2, tp // 2, tp % 2


def seq_of(z, y, x_lo):
    return z * 8 + y * 2 + x_lo


def x_neighbours():
    z, y, x_lo, x_hi, core = places()
    x = x_hi * 2 + x_lo
    ids = []
    for step in (1, 3):
        other = lax.rem(x + step, 4)
        ids.append((seq_of(z, y, other % 2), (other // 2) * 2 + core))
    return x, ids


def greet(ids):
    barrier = pltpu.get_barrier_semaphore()
    for one in ids:
        pl.semaphore_signal(barrier, inc=1, device_id=one, device_id_type=MESH)
    pl.semaphore_wait(barrier, len(ids))


def remote(src, dst, send, recv, target):
    return pltpu.make_async_remote_copy(
        src_ref=src, dst_ref=dst, send_sem=send, recv_sem=recv, device_id=target,
        device_id_type=MESH,
    )


CHUNKS = 6
CHUNK = BLOCK // CHUNKS
TILE_SLOTS = N_SEQ // N_TILES
TILE = TILE_SLOTS * BLOCK
LAST_BLOCK = 2 * N_SEQ - 1
KV_COLS = 2 * HD


def layer_kernel(
    short_lengths, hidden, gain, frequency, page_slot, wq, wk, wv, w_out, out, pages,
    xbuf, relay, wbuf, wout, fbuf, total, cosine, sine, first_b, q, kv, buf, m_ref, l_ref, acc_ref,
    attended, sendp, recvp, sendx, recvx, relay_out,
    load_sem, send_sem, r0, r1, r2, r3, own_sem, seq_send, seq_recv, out_send, rp, o1, o2,
):
    z, y, x_lo, x_hi, core = places()
    seq = lax.axis_index("seq")
    tp = lax.axis_index("tp")
    loads = [
        pltpu.make_async_copy(hidden, xbuf.at[tp], load_sem.at[0]),
        pltpu.make_async_copy(wk, wbuf.at[:, 0:HD], load_sem.at[1]),
        pltpu.make_async_copy(wv, wbuf.at[:, HD:KV_COLS], load_sem.at[2]),
        pltpu.make_async_copy(wq, wbuf.at[:, KV_COLS:], load_sem.at[3]),
        pltpu.make_async_copy(frequency, fbuf, load_sem.at[4]),
        pltpu.make_async_copy(w_out, wout, load_sem.at[5]),
    ]
    for one in loads:
        one.start()
    x, sides = x_neighbours()
    partner = (seq, x_hi * 2 + 1 - core)
    target = {
        "x": (seq_of(z, y, 1 - x_lo), tp),
        "y+": (seq_of(z, lax.rem(y + 1, 4), x_lo), tp),
        "y-": (seq_of(z, lax.rem(y + 3, 4), x_lo), tp),
        "z+": (seq_of(lax.rem(z + 1, 8), y, x_lo), tp),
        "z-": (seq_of(lax.rem(z + 7, 8), y, x_lo), tp),
    }
    greet([partner] + sides + [target[link] for link in ("y+", "y-", "z+", "z-")])

    sends = []

    def go(copy):
        copy.start()
        sends.append(copy)
        return copy

    def rows_of(k):
        return pl.ds(k * CHUNK, CHUNK)

    opposite = (1 - x_hi) * 2 + core
    loads[0].wait()
    firsts = {}
    for c in range(CHUNKS):
        for way in range(2):
            k = way * CHUNKS + c
            firsts[k] = go(
                remote(xbuf.at[tp, rows_of(k)], relay.at[k], send_sem.at[k], r1.at[k], sides[way])
            )
    own = go(remote(xbuf.at[tp], xbuf.at[tp], send_sem.at[6 * CHUNKS], r0, partner))

    def pass_on(k):
        way = k // CHUNKS
        firsts[k].wait_recv()
        source = lax.rem(x + (3 if way == 0 else 1), 4)
        go(
            remote(
                relay.at[k], xbuf.at[(source // 2) * 2 + core, rows_of(k)],
                send_sem.at[2 * CHUNKS + k], r2.at[k], sides[way],
            )
        )

    thirds = {}

    def share(k):
        here = xbuf.at[opposite, rows_of(k)]
        remote(
            relay.at[k], here, send_sem.at[2 * CHUNKS + k], r2.at[k], sides[k // CHUNKS]
        ).wait_recv()
        thirds[k] = go(remote(here, here, send_sem.at[4 * CHUNKS + k], r3.at[k], partner))

    def scaled(part):
        wide = xbuf[part].astype(F32)
        squares = jnp.sum(wide * wide, axis=1, keepdims=True)
        cols = pl.ds(pl.multiple_of(part * COLS, COLS), COLS)
        return squares, (wide * gain[:, cols].astype(F32)).astype(BF16), cols

    def whole_part(part, first):
        squares, rows, cols = scaled(part)
        product = jnp.dot(rows, wbuf[cols, :], preferred_element_type=F32)
        total[...] = product if first else total[...] + product
        return squares

    def facts():
        row = lax.broadcasted_iota(jnp.int32, (BLOCK, HD), 0)
        lane = lax.broadcasted_iota(jnp.int32, (BLOCK, HD), 1)
        sign = jnp.where(lane < HD // 2, -1.0, 1.0).astype(F32)
        for half in range(2):
            pos = row + (seq if half == 0 else LAST_BLOCK - seq) * BLOCK
            first = jnp.zeros((BLOCK, HD), jnp.int32)
            bound = LONG
            for j in range(short_lengths.shape[0]):
                first = jnp.where(pos >= bound, bound, first)
                bound = bound + short_lengths[j]
            angles = (pos - first).astype(F32) * fbuf[...]
            cosine[half] = jnp.cos(angles)
            sine[half] = jnp.sin(angles) * sign
            if half == 1:
                first_b[...] = first[:, :1]

    for one in loads[1:5]:
        one.wait()
    squares = whole_part(tp, True)
    for c in range(CHUNKS):
        for way in range(2):
            pass_on(way * CHUNKS + c)
        if c == 0:
            own.wait_recv()
            squares = squares + whole_part(x_hi * 2 + 1 - core, False)
        if c == 1:
            facts()
        if c >= 1:
            for way in range(2):
                share(way * CHUNKS + c - 1)
    for way in range(2):
        share(way * CHUNKS + CHUNKS - 1)
    late = []
    for part in (opposite, (1 - x_hi) * 2 + 1 - core):
        if late:
            for k in range(2 * CHUNKS):
                thirds[k].wait_recv()
        more, rows, cols = scaled(part)
        squares = squares + more
        late.append((rows, cols))
        total[:, :KV_COLS] += jnp.dot(rows, wbuf[cols, :KV_COLS], preferred_element_type=F32)
    factor = lax.rsqrt(squares * (1.0 / D) + norm_eps)

    def turned(half, cols):
        rows = slice(half * BLOCK, (half + 1) * BLOCK)
        u = total[rows, cols] * factor[rows]
        return (u * cosine[half] + pltpu.roll(u, HD // 2, 1) * sine[half]).astype(BF16)

    for half in range(2):
        rows = slice(half * BLOCK, (half + 1) * BLOCK)
        kv[half] = turned(half, slice(0, HD)).reshape(BLOCK // THIRD, THIRD, HD)
        kv[2 + half] = (
            (total[rows, HD:KV_COLS] * factor[rows])
            .astype(BF16)
            .reshape(BLOCK // THIRD, THIRD, HD)
        )

    def chunk(color, off):
        dz, dy, dx = off
        slot = seq_of(
            lax.rem(z + (dz + 8), 8), lax.rem(y + (dy + 4), 4), x_lo if dx == 0 else 1 - x_lo
        )
        return buf.at[:, slot, color]

    def send(color, off, link, src):
        there = shifted(off, link)
        remote(
            src, chunk(color, off), seq_send.at[color],
            seq_recv.at[color, OFFSETS.index(there)], target[link],
        ).start()

    def take(batch):
        for color, off, links in batch:
            here = chunk(color, off)
            remote(
                here, here, seq_send.at[color], seq_recv.at[color, OFFSETS.index(off)], target["x"]
            ).wait_recv()
            for link in links:
                send(color, off, link, here)

    own_copy = pltpu.make_async_copy(kv, buf.at[:, seq], own_sem)
    own_copy.start()
    for color in range(3):
        for link in onward(color, (0, 0, 0), "own"):
            send(color, (0, 0, 0), link, kv.at[:, color])
    for rows, cols in late:
        total[:, KV_COLS:] += jnp.dot(rows, wbuf[cols, KV_COLS:], preferred_element_type=F32)
    for head in range(GROUP):
        for half in range(2):
            q[half, head] = turned(half, slice(KV_COLS + head * HD, KV_COLS + (head + 1) * HD))
    m_ref[...] = jnp.full(m_ref.shape, NEG, F32)
    l_ref[...] = jnp.zeros(l_ref.shape, F32)
    acc_ref[...] = jnp.zeros(acc_ref.shape, F32)
    own_copy.wait()

    def step(half, region, tile, allowed):
        rows = pl.ds(tile * TILE_SLOTS, TILE_SLOTS)
        keys = buf[region, rows].reshape(TILE, HD)
        values = buf[2 + region, rows].reshape(TILE, HD)
        for head in range(GROUP):
            scores = lax.dot_general(
                q[half, head], keys, (((1,), (1,)), ((), ())), preferred_element_type=F32
            )
            if allowed is not None:
                scores = jnp.where(allowed, scores, NEG)
            old = m_ref[half, head]
            new = jnp.maximum(old, jnp.max(scores, axis=1, keepdims=True))
            weights = jnp.exp2(scores * SCALE2 - new * SCALE2)
            if allowed is not None:
                weights = jnp.where(allowed, weights, 0.0)
            keep = jnp.exp2((old - new) * SCALE2)
            m_ref[half, head] = new
            l_ref[half, head] = l_ref[half, head] * keep + jnp.sum(weights, axis=1, keepdims=True)
            acc_ref[half, head] = acc_ref[half, head] * keep + jnp.dot(
                weights.astype(BF16), values, preferred_element_type=F32
            )

    def masked_a(tile):
        row = lax.broadcasted_iota(jnp.int32, (BLOCK, TILE), 0)
        col = lax.broadcasted_iota(jnp.int32, (BLOCK, TILE), 1)
        step(0, 0, tile, col + tile * TILE <= row + seq * BLOCK)

    def masked_b(tile):
        row = lax.broadcasted_iota(jnp.int32, (BLOCK, TILE), 0)
        col = lax.broadcasted_iota(jnp.int32, (BLOCK, TILE), 1)
        slot_in = sum((col >= n * BLOCK).astype(jnp.int32) for n in range(1, TILE_SLOTS))
        key_pos = col - 2 * BLOCK * slot_in + (LAST_BLOCK - tile * TILE_SLOTS) * BLOCK
        row_pos = row + (LAST_BLOCK - seq) * BLOCK
        step(1, 1, tile, (key_pos <= row_pos) & (key_pos >= first_b[...]))

    own_tile = seq // TILE_SLOTS
    in_long = (seq + (LONG_BLOCKS - N_SEQ)) // N_SEQ
    short_end = (seq + 6) // TILE_SLOTS

    def batch_at(unit, part):
        for k in range(N_TILES):
            batch = BATCHES[3 * k + part]
            if batch:
                pl.when(unit == k)(functools.partial(take, batch))

    @pl.loop(0, N_TILES)
    def _(unit):
        rank = unit // 2
        dz = (rank + 1) // 2 * (1 - 2 * ((rank + 1) % 2))
        tile = (z + dz + 8) % 8 * 2 + (y // 2 + unit % 2) % 2
        batch_at(unit, 0)

        @pl.when(in_long == 1)
        def _():
            step(1, 0, tile, None)

        batch_at(unit, 1)

        @pl.when(tile < own_tile)
        def _():
            step(0, 0, tile, None)

        @pl.when(tile == own_tile)
        def _():
            masked_a(tile)

        batch_at(unit, 2)

        @pl.when((in_long == 1) & (tile > own_tile))
        def _():
            step(1, 1, tile, None)

        @pl.when((tile == own_tile) | ((in_long == 0) & (tile > own_tile) & (tile <= short_end)))
        def _():
            masked_b(tile)

    for half in range(2):
        for head in range(GROUP):
            attended[half * BLOCK : (half + 1) * BLOCK, head * HD : (head + 1) * HD] = (
                acc_ref[half, head] / l_ref[half, head]
            ).astype(BF16)

    loads[5].wait()
    far = (1 - x_hi) * 2
    near = x_hi * 2

    def terms(part, way):
        cols = pl.ds(pl.multiple_of(part * COLS, COLS), COLS)
        rows = slice(way * BLOCK, (way + 1) * BLOCK)
        return jnp.dot(attended[rows, :], wout[:, cols], preferred_element_type=F32)

    def to_partner(which, way, part):
        rows = pl.ds(way * BLOCK, BLOCK)
        sendp[which, rows] = terms(part, way).astype(BF16)
        k = 2 * which + way
        return go(
            remote(
                sendp.at[which, rows], recvp.at[which, rows], out_send.at[4 * CHUNKS + k],
                rp.at[k], partner,
            )
        )

    far_copies = [to_partner(0, way, far + 1 - core) for way in range(2)]
    hops = {}
    for way in range(2):
        rows = pl.ds(way * BLOCK, BLOCK)
        mine = terms(far + core, way)
        far_copies[way].wait_recv()
        sendx[rows] = (mine + recvp[0, rows].astype(F32)).astype(BF16)
        for c in range(CHUNKS):
            k = way * CHUNKS + c
            hops[k] = go(
                remote(sendx.at[rows_of(k)], relay_out.at[k], out_send.at[k], o1.at[k], sides[way])
            )
    near_copies = [to_partner(1, way, near + 1 - core) for way in range(2)]
    lands = {}
    for c in range(CHUNKS):
        for way in range(2):
            k = way * CHUNKS + c
            hops[k].wait_recv()
            lands[k] = go(
                remote(
                    relay_out.at[k], recvx.at[rows_of(k)], out_send.at[2 * CHUNKS + k], o2.at[k],
                    sides[way],
                )
            )
    for page in range(ROWS // PAGE):
        ids = lax.broadcasted_iota(jnp.int32, page_slot.shape, 0) * page_slot.shape[
            1
        ] + lax.broadcasted_iota(jnp.int32, page_slot.shape, 1)
        name = jnp.max(jnp.where(page_slot[...] == seq * (ROWS // PAGE) + page, ids, 0))
        block = name // (BLOCK // PAGE)
        part = name - block * (BLOCK // PAGE)
        region = block // N_SEQ
        slot = block + region * (LAST_BLOCK - 2 * block)
        pages[page, 0] = buf[region, slot, part]
        pages[page, 1] = buf[region + 2, slot, part]
    own_x = xbuf[tp].astype(F32)
    for way in range(2):
        rows = slice(way * BLOCK, (way + 1) * BLOCK)
        kept = terms(near + core, way) + own_x[rows]
        near_copies[way].wait_recv()
        kept = kept + recvp[1, rows].astype(F32)
        for c in range(CHUNKS):
            lands[way * CHUNKS + c].wait_recv()
        out[rows, :] = (kept + recvx[rows].astype(F32)).astype(BF16)
    for one in sends:
        one.wait_send()
    for color in range(3):
        sent = buf.at[:, pl.ds(0, N_SEQ - 1), color]
        pltpu.make_async_copy(sent, sent, seq_send.at[color]).wait()


VM = pl.BlockSpec(memory_space=pltpu.VMEM)
SM = pl.BlockSpec(memory_space=pltpu.SMEM)
ANY = pl.BlockSpec(memory_space=pl.ANY)
DMA = pltpu.SemaphoreType.DMA


def local(hidden_in, norm_gain, w_query, w_key, w_value, w_out, short_lengths, page_slot):
    half = np.arange(HD // 2, dtype=np.float32)
    frequency = np.float32(rope_base) ** (-(half * np.float32(2.0)) / np.float32(HD))
    frequency = np.concatenate([frequency, frequency]).astype(np.float32).reshape(1, HD)
    return pl.pallas_call(
        layer_kernel,
        out_shape=(
            jax.ShapeDtypeStruct((ROWS, COLS), BF16),
            jax.ShapeDtypeStruct((ROWS // PAGE, 2, PAGE, HD), BF16),
        ),
        in_specs=[SM, ANY, VM, ANY, VM, ANY, ANY, ANY, ANY],
        out_specs=(VM, VM),
        scratch_shapes=[
            pltpu.VMEM((N_TP, ROWS, COLS), BF16),
            pltpu.VMEM((2 * CHUNKS, CHUNK, COLS), BF16),
            pltpu.VMEM((D, KV_COLS + HEAD_COLS), BF16),
            pltpu.VMEM((HEAD_COLS, D), BF16),
            pltpu.VMEM((1, HD), F32),
            pltpu.VMEM((ROWS, KV_COLS + HEAD_COLS), F32),
            pltpu.VMEM((2, BLOCK, HD), F32),
            pltpu.VMEM((2, BLOCK, HD), F32),
            pltpu.VMEM((BLOCK, 1), jnp.int32),
            pltpu.VMEM((2, GROUP, BLOCK, HD), BF16),
            pltpu.VMEM((4, BLOCK // THIRD, THIRD, HD), BF16),
            pltpu.VMEM((4, N_SEQ, BLOCK // THIRD, THIRD, HD), BF16),
            pltpu.VMEM((2, GROUP, BLOCK, 1), F32),
            pltpu.VMEM((2, GROUP, BLOCK, 1), F32),
            pltpu.VMEM((2, GROUP, BLOCK, HD), F32),
            pltpu.VMEM((ROWS, HEAD_COLS), BF16),
            pltpu.VMEM((2, ROWS, COLS), BF16),
            pltpu.VMEM((2, ROWS, COLS), BF16),
            pltpu.VMEM((ROWS, COLS), BF16),
            pltpu.VMEM((ROWS, COLS), BF16),
            pltpu.VMEM((2 * CHUNKS, CHUNK, COLS), BF16),
            DMA((6,)),
            DMA((6 * CHUNKS + 1,)),
            DMA(()),
            DMA((2 * CHUNKS,)),
            DMA((2 * CHUNKS,)),
            DMA((2 * CHUNKS,)),
            DMA(()),
            DMA((3,)),
            DMA((3, len(OFFSETS))),
            DMA((4 * CHUNKS + 4,)),
            DMA((4,)),
            DMA((2 * CHUNKS,)),
            DMA((2 * CHUNKS,)),
        ],
        compiler_params=pltpu.CompilerParams(
            collective_id=0, has_side_effects=True, vmem_limit_bytes=60 * 1024 * 1024
        ),
        name="layer",
    )(
        short_lengths,
        hidden_in,
        norm_gain.reshape(1, D),
        jnp.asarray(frequency),
        page_slot.reshape(-1, HD),
        w_query,
        w_key,
        w_value,
        w_out,
    )


def solution(mesh):
    placed = (
        P("seq", "tp"),
        P(),
        P(None, "tp"),
        P(None, "tp"),
        P(None, "tp"),
        P("tp", None),
        P(),
        P(),
    )
    return jax.shard_map(
        local,
        mesh=mesh,
        in_specs=placed,
        out_specs=(P("seq", "tp"), P("seq", None, None, "tp")),
        check_vma=False,
    )
```

time: 178 us -> 143 us (0.80)
  Pallas kernels: 163 us -> 138 us
  local copies, waits for them, and re-layouts: 10.7 us -> 4.83 us
  other arithmetic: 3.55 us -> 0 us
    pallas_call x3 -> x1, Pallas kernels: 163 us -> 138 us  [local(): pl.pallas_call(layer_kernel, out_shape=(jax.ShapeDtypeStruct((ROWS, COLS)...]
    unnamed x22 -> x2, local copies, waits for them, and re-layouts: 8.83 us -> 3.53 us
where the time goes in v2:
time: 143 us
  Pallas kernels  138 us (97%)
  local copies, waits for them, and re-layouts  4.83 us (3%)
    pallas_call x1, Pallas kernels, local(): pl.pallas_call(layer_kernel, out_shape=(jax.ShapeDtypeStruct((ROWS, COLS)...  138 us
    unnamed x2, local copies, waits for them, and re-layouts  3.53 us

profile of v2, /device:TPU:193, one launch (start us, length us, event | category | flops | bytes accessed | tf_op | source)
XLA Modules:
  0.0 143.1 jit_solution(14053863912745260903)
XLA Ops:
  0.6 1.3 reshape.10.gain
  1.9 137.7 %layer.1 = (bf16[384,768]{1,0:T(8,128)(2,1)}, bf16[6,2,64,128]{3,2,1,0:T(8,128)(2,1)}) custom-call(s32[14]{0:T(128)} %short_lengths.1, bf16[384,768]{1,0:T(8,128)(2,1)} %hidden.1, bf16[1,3072]{1,0:T(2,128)(2,1)} %reshape.10.gain, f32[1,128]{1,0:T(1,128)} %constant.2.clone.frequency, s32[3,128]{1,0:T(4,128)} %bitcast.1, bf16[3072,384]{1,0:T(8,128)(2,1)} %wq.1, ...), custom_call_target="tpu_custom_call" | custom-call | tf_op jit(solution)/shard_map/layer/pallas_call | solution.py:506
  139.6 1.9 %copy.13 = bf16[384,768]{1,0:T(8,128)(2,1)} copy(bf16[384,768]{1,0:T(8,128)(2,1)} %get-tuple-element.4) | data formatting | bytes 1179648
  141.5 1.6 %copy.14 = bf16[6,2,64,128]{3,2,1,0:T(8,128)(2,1)} copy(bf16[6,2,64,128]{3,2,1,0:T(8,128)(2,1)} %get-tuple-element.5) | data formatting | bytes 393216

commit v3 on v2

--- a/solution.py
+++ b/solution.py
@@ -65,7 +65,7 @@
     return (4 if dz == -4 else dz, 2 if dy == -2 else dy, dx)
 
 
-def plan(copy_us=1.41, hop_us=1.7, step_us=1.0, first_us=1.5):
+def plan(copy_us=1.41, hop_us=1.7, step_us=1.3, first_us=1.5):
     free, heap, count, now = {}, [], 0, 0.0
 
     def issue(color, off, links):
@@ -83,8 +83,8 @@
     now = first_us
     missing = [set() for _ in range(STEPS // 3)]
     for unit in range(STEPS // 3):
-        dz = plane_of(unit // 2)
-        for dy in (0, 1, -1, 2) if unit % 2 else (0, 1, -1):
+        dz = plane_of(unit)
+        for dy in (0, 1, -1, 2):
             for dx in (0, 1):
                 missing[unit] |= {(color, (dz, dy, dx)) for color in range(3)}
         missing[unit] -= {(color, (0, 0, 0)) for color in range(3)}
@@ -107,8 +107,8 @@
     return batches, now
 
 
-N_TILES = 16
-STEPS = 3 * N_TILES
+N_PLANES = 8
+STEPS = 3 * N_PLANES
 
 
 def plane_of(rank):
@@ -155,8 +155,11 @@
 
 CHUNKS = 6
 CHUNK = BLOCK // CHUNKS
-TILE_SLOTS = N_SEQ // N_TILES
-TILE = TILE_SLOTS * BLOCK
+SLOTS = N_SEQ // N_PLANES
+KEYS = SLOTS * BLOCK
+PIECES = 2
+PIECE = KEYS // PIECES
+QUERIES = GROUP * BLOCK
 LAST_BLOCK = 2 * N_SEQ - 1
 KV_COLS = 2 * HD
 
@@ -244,6 +247,10 @@
         total[...] = product if first else total[...] + product
         return squares
 
+    def lane_row(shape):
+        lane = lax.broadcasted_iota(jnp.int32, shape, 1)
+        return lane - BLOCK * sum((lane >= n * BLOCK).astype(jnp.int32) for n in range(1, GROUP))
+
     def facts():
         row = lax.broadcasted_iota(jnp.int32, (BLOCK, HD), 0)
         lane = lax.broadcasted_iota(jnp.int32, (BLOCK, HD), 1)
@@ -258,8 +265,13 @@
             angles = (pos - first).astype(F32) * fbuf[...]
             cosine[half] = jnp.cos(angles)
             sine[half] = jnp.sin(angles) * sign
-            if half == 1:
-                first_b[...] = first[:, :1]
+        pos = lane_row((1, QUERIES)) + (LAST_BLOCK - seq) * BLOCK
+        first = jnp.zeros((1, QUERIES), jnp.int32)
+        bound = LONG
+        for j in range(short_lengths.shape[0]):
+            first = jnp.where(pos >= bound, bound, first)
+            bound = bound + short_lengths[j]
+        first_b[...] = first
 
     for one in loads[1:5]:
         one.wait()
@@ -334,93 +346,108 @@
         total[:, KV_COLS:] += jnp.dot(rows, wbuf[cols, KV_COLS:], preferred_element_type=F32)
     for head in range(GROUP):
         for half in range(2):
-            q[half, head] = turned(half, slice(KV_COLS + head * HD, KV_COLS + (head + 1) * HD))
+            q[half, head * BLOCK : (head + 1) * BLOCK] = turned(
+                half, slice(KV_COLS + head * HD, KV_COLS + (head + 1) * HD)
+            )
     m_ref[...] = jnp.full(m_ref.shape, NEG, F32)
     l_ref[...] = jnp.zeros(l_ref.shape, F32)
     acc_ref[...] = jnp.zeros(acc_ref.shape, F32)
     own_copy.wait()
 
-    def step(half, region, tile, allowed):
-        rows = pl.ds(tile * TILE_SLOTS, TILE_SLOTS)
-        keys = buf[region, rows].reshape(TILE, HD)
-        values = buf[2 + region, rows].reshape(TILE, HD)
-        for head in range(GROUP):
-            scores = lax.dot_general(
-                q[half, head], keys, (((1,), (1,)), ((), ())), preferred_element_type=F32
-            )
+    def step(half, region, plane, allowed):
+        slots = pl.ds(plane * SLOTS, SLOTS)
+        keys = buf[region, slots].reshape(KEYS, HD)
+        values = buf[2 + region, slots].reshape(KEYS, HD)
+        queries = q[half]
+        pieces = [slice(n * PIECE, (n + 1) * PIECE) for n in range(PIECES)]
+        scores = []
+        for n, piece in enumerate(pieces):
+            one = lax.dot_general(
+                keys[piece], queries, (((1,), (1,)), ((), ())), preferred_element_type=F32
+            )
+            scores.append(one if allowed is None else jnp.where(allowed(n), one, NEG))
+        old = m_ref[half]
+        new = old
+        for one in scores:
+            new = jnp.maximum(new, jnp.max(one, axis=0, keepdims=True))
+        shift = new * SCALE2
+        keep = jnp.exp2(old * SCALE2 - shift)
+        m_ref[half] = new
+        denominator = l_ref[half] * keep
+        numerator = acc_ref[half] * keep
+        for n, piece in enumerate(pieces):
+            weights = jnp.exp2(scores[n] * SCALE2 - shift)
             if allowed is not None:
-                scores = jnp.where(allowed, scores, NEG)
-            old = m_ref[half, head]
-            new = jnp.maximum(old, jnp.max(scores, axis=1, keepdims=True))
-            weights = jnp.exp2(scores * SCALE2 - new * SCALE2)
-            if allowed is not None:
-                weights = jnp.where(allowed, weights, 0.0)
-            keep = jnp.exp2((old - new) * SCALE2)
-            m_ref[half, head] = new
-            l_ref[half, head] = l_ref[half, head] * keep + jnp.sum(weights, axis=1, keepdims=True)
-            acc_ref[half, head] = acc_ref[half, head] * keep + jnp.dot(
-                weights.astype(BF16), values, preferred_element_type=F32
-            )
-
-    def masked_a(tile):
-        row = lax.broadcasted_iota(jnp.int32, (BLOCK, TILE), 0)
-        col = lax.broadcasted_iota(jnp.int32, (BLOCK, TILE), 1)
-        step(0, 0, tile, col + tile * TILE <= row + seq * BLOCK)
-
-    def masked_b(tile):
-        row = lax.broadcasted_iota(jnp.int32, (BLOCK, TILE), 0)
-        col = lax.broadcasted_iota(jnp.int32, (BLOCK, TILE), 1)
-        slot_in = sum((col >= n * BLOCK).astype(jnp.int32) for n in range(1, TILE_SLOTS))
-        key_pos = col - 2 * BLOCK * slot_in + (LAST_BLOCK - tile * TILE_SLOTS) * BLOCK
-        row_pos = row + (LAST_BLOCK - seq) * BLOCK
-        step(1, 1, tile, (key_pos <= row_pos) & (key_pos >= first_b[...]))
-
-    own_tile = seq // TILE_SLOTS
+                weights = jnp.where(allowed(n), weights, 0.0)
+            denominator = denominator + jnp.sum(weights, axis=0, keepdims=True)
+            numerator = numerator + lax.dot_general(
+                values[piece], weights.astype(BF16), (((0,), (0,)), ((), ())),
+                preferred_element_type=F32,
+            )
+        l_ref[half] = denominator
+        acc_ref[half] = numerator
+
+    def masked_a(plane):
+        def allowed(n):
+            key = lax.broadcasted_iota(jnp.int32, (PIECE, 1), 0) + (n * PIECE + plane * KEYS)
+            return key <= lane_row((1, QUERIES)) + seq * BLOCK
+
+        step(0, 0, plane, allowed)
+
+    def masked_b(plane):
+        def allowed(n):
+            row = lax.broadcasted_iota(jnp.int32, (PIECE, 1), 0) + n * PIECE
+            slot_in = sum((row >= k * BLOCK).astype(jnp.int32) for k in range(1, SLOTS))
+            key = row - 2 * BLOCK * slot_in + (LAST_BLOCK - plane * SLOTS) * BLOCK
+            query = lane_row((1, QUERIES)) + (LAST_BLOCK - seq) * BLOCK
+            return (key <= query) & (key >= first_b[...])
+
+        step(1, 1, plane, allowed)
+
     in_long = (seq + (LONG_BLOCKS - N_SEQ)) // N_SEQ
-    short_end = (seq + 6) // TILE_SLOTS
 
     def batch_at(unit, part):
-        for k in range(N_TILES):
+        for k in range(N_PLANES):
             batch = BATCHES[3 * k + part]
             if batch:
                 pl.when(unit == k)(functools.partial(take, batch))
 
-    @pl.loop(0, N_TILES)
+    @pl.loop(0, N_PLANES)
     def _(unit):
-        rank = unit // 2
-        dz = (rank + 1) // 2 * (1 - 2 * ((rank + 1) % 2))
-        tile = (z + dz + 8) % 8 * 2 + (y // 2 + unit % 2) % 2
+        dz = (unit + 1) // 2 * (1 - 2 * ((unit + 1) % 2))
+        plane = (z + dz + 8) % 8
         batch_at(unit, 0)
 
         @pl.when(in_long == 1)
         def _():
-            step(1, 0, tile, None)
+            step(1, 0, plane, None)
 
         batch_at(unit, 1)
 
-        @pl.when(tile < own_tile)
+        @pl.when(plane < z)
         def _():
-            step(0, 0, tile, None)
-
-        @pl.when(tile == own_tile)
+            step(0, 0, plane, None)
+
+        @pl.when(plane == z)
         def _():
-            masked_a(tile)
+            masked_a(plane)
 
         batch_at(unit, 2)
 
-        @pl.when((in_long == 1) & (tile > own_tile))
+        @pl.when((in_long == 1) & (plane > z))
         def _():
-            step(1, 1, tile, None)
-
-        @pl.when((tile == own_tile) | ((in_long == 0) & (tile > own_tile) & (tile <= short_end)))
+            step(1, 1, plane, None)
+
+        @pl.when((plane == z) | ((in_long == 0) & (plane == z + 1)))
         def _():
-            masked_b(tile)
+            masked_b(plane)
 
     for half in range(2):
+        ready = jnp.transpose(acc_ref[half] / l_ref[half]).astype(BF16)
         for head in range(GROUP):
-            attended[half * BLOCK : (half + 1) * BLOCK, head * HD : (head + 1) * HD] = (
-                acc_ref[half, head] / l_ref[half, head]
-            ).astype(BF16)
+            attended[half * BLOCK : (half + 1) * BLOCK, head * HD : (head + 1) * HD] = ready[
+                head * BLOCK : (head + 1) * BLOCK
+            ]
 
     loads[5].wait()
     far = (1 - x_hi) * 2
@@ -520,13 +547,13 @@
             pltpu.VMEM((ROWS, KV_COLS + HEAD_COLS), F32),
             pltpu.VMEM((2, BLOCK, HD), F32),
             pltpu.VMEM((2, BLOCK, HD), F32),
-            pltpu.VMEM((BLOCK, 1), jnp.int32),
-            pltpu.VMEM((2, GROUP, BLOCK, HD), BF16),
+            pltpu.VMEM((1, QUERIES), jnp.int32),
+            pltpu.VMEM((2, QUERIES, HD), BF16),
             pltpu.VMEM((4, BLOCK // THIRD, THIRD, HD), BF16),
             pltpu.VMEM((4, N_SEQ, BLOCK // THIRD, THIRD, HD), BF16),
-            pltpu.VMEM((2, GROUP, BLOCK, 1), F32),
-            pltpu.VMEM((2, GROUP, BLOCK, 1), F32),
-            pltpu.VMEM((2, GROUP, BLOCK, HD), F32),
+            pltpu.VMEM((2, 1, QUERIES), F32),
+            pltpu.VMEM((2, 1, QUERIES), F32),
+            pltpu.VMEM((2, HD, QUERIES), F32),
             pltpu.VMEM((ROWS, HEAD_COLS), BF16),
             pltpu.VMEM((2, ROWS, COLS), BF16),
             pltpu.VMEM((2, ROWS, COLS), BF16),

time: 143 us -> 127 us (0.89)
  Pallas kernels: 138 us -> 121 us
    pallas_call x1, Pallas kernels: 138 us -> 121 us  [local(): pl.pallas_call(layer_kernel, out_shape=(jax.ShapeDtypeStruct((ROWS, COLS)...]
where the time goes in v3:
time: 127 us
  Pallas kernels  121 us (95%)
  local copies, waits for them, and re-layouts  4.83 us (4%)
    pallas_call x1, Pallas kernels, local(): pl.pallas_call(layer_kernel, out_shape=(jax.ShapeDtypeStruct((ROWS, COLS)...  121 us
    unnamed x2, local copies, waits for them, and re-layouts  3.53 us

profile of v3, /device:TPU:193, one launch (start us, length us, event | category | flops | bytes accessed | tf_op | source)
XLA Modules:
  0.0 126.9 jit_solution(1117301204422057971)
XLA Ops:
  0.6 1.3 %reshape.10.gain = bf16[1,3072]{1,0:T(2,128)(2,1)} reshape(bf16[3072]{0:T(1024)(128)(2,1)} %param.10) | data formatting | bytes 12288 | tf_op jit(solution)/shard_map/reshape | solution.py:584
  1.9 121.4 %layer.1 = (bf16[384,768]{1,0:T(8,128)(2,1)}, bf16[6,2,64,128]{3,2,1,0:T(8,128)(2,1)}) custom-call(s32[14]{0:T(128)} %short_lengths.1, bf16[384,768]{1,0:T(8,128)(2,1)} %hidden.1, bf16[1,3072]{1,0:T(2,128)(2,1)} %reshape.10.gain, f32[1,128]{1,0:T(1,128)} %constant.2.clone.frequency, s32[3,128]{1,0:T(4,128)} %bitcast.1, bf16[3072,384]{1,0:T(8,128)(2,1)} %wq.1, ...), custom_call_target="tpu_custom_call" | custom-call | tf_op jit(solution)/shard_map/layer/pallas_call | solution.py:533
  123.3 1.9 %copy.13 = bf16[384,768]{1,0:T(8,128)(2,1)} copy(bf16[384,768]{1,0:T(8,128)(2,1)} %get-tuple-element.4) | data formatting | bytes 1179648
  125.2 1.6 %copy.14 = bf16[6,2,64,128]{3,2,1,0:T(8,128)(2,1)} copy(bf16[6,2,64,128]{3,2,1,0:T(8,128)(2,1)} %get-tuple-element.5) | data formatting | bytes 393216

commit v4 on v3

--- a/solution.py
+++ b/solution.py
@@ -65,58 +65,97 @@
     return (4 if dz == -4 else dz, 2 if dy == -2 else dy, dx)
 
 
-def plan(copy_us=1.41, hop_us=1.7, step_us=1.3, first_us=1.5):
-    free, heap, count, now = {}, [], 0, 0.0
-
-    def issue(color, off, links):
+N_PLANES = 8
+STEPS = 3 * N_PLANES
+STARTS = (2, 0, 1)
+START_US = (0.0, 4.2, 6.3)
+CUTS = (0.5, 3.2, 4.7, 5.0, 6.8)
+
+
+def plane_of(rank):
+    return (rank + 1) // 2 * (1 - 2 * ((rank + 1) % 2))
+
+
+def timetable(copy_us=1.41, hop_us=1.7, ahead_us=4.0):
+    heap, count, queues, busy, arrived, served = [], 0, {}, {}, {}, []
+
+    def put(now, what):
         nonlocal count
-        for link in links:
-            first = max(now, free.get(link, 0.0))
-            free[link] = first + copy_us
+        count += 1
+        heapq.heappush(heap, (now, count, what))
+
+    def kick(link, now):
+        if busy.get(link, 0.0) > now + 1e-6 or not queues.get(link):
+            return
+        _, _, color, off = heapq.heappop(queues[link])
+        busy[link] = now + copy_us
+        served.append((now, color, off, link))
+        put(now + copy_us, (link,))
+        put(now + copy_us + hop_us, (color, shifted(off, link), link))
+
+    for color, start in zip(STARTS, START_US):
+        put(start, (color, (0, 0, 0), "own"))
+    while heap:
+        now, order, what = heapq.heappop(heap)
+        if len(what) == 1:
+            kick(what[0], now)
+            continue
+        color, off, via = what
+        arrived[color, off] = now
+        for link in onward(color, off, via):
             count += 1
-            heapq.heappush(
-                heap, (first + copy_us + hop_us, count, color, shifted(off, link), link)
-            )
-
-    for color in range(3):
-        issue(color, (0, 0, 0), onward(color, (0, 0, 0), "own"))
-    now = first_us
-    missing = [set() for _ in range(STEPS // 3)]
-    for unit in range(STEPS // 3):
+            heapq.heappush(queues.setdefault(link, []), (abs(off[0]), count, color, off))
+            kick(link, now)
+    actions = [(now, 0, one, None) for one, now in arrived.items() if one[1] != (0, 0, 0)]
+    last = {}
+    for start, color, off, link in served:
+        due = max(arrived[color, off], start - ahead_us, last.get(link, 0.0))
+        last[link] = due
+        actions.append((due, 1, (color, off), link))
+    actions.sort(key=lambda one: one[:2])
+    return actions
+
+
+def plan(step_us=1.2, first_us=1.5):
+    actions = timetable()
+    early = []
+    for cut in CUTS:
+        early.append([one for one in actions if one[0] <= cut])
+        actions = actions[len(early[-1]) :]
+    missing = []
+    for unit in range(N_PLANES):
         dz = plane_of(unit)
-        for dy in (0, 1, -1, 2):
-            for dx in (0, 1):
-                missing[unit] |= {(color, (dz, dy, dx)) for color in range(3)}
-        missing[unit] -= {(color, (0, 0, 0)) for color in range(3)}
-    taken, batches, batch, step = set(), [], [], 0
-    while step < STEPS or heap:
-        if heap and heap[0][0] <= now:
-            _, _, color, off, link = heapq.heappop(heap)
-            links = onward(color, off, link)
-            taken.add((color, off))
-            batch.append((color, off, links))
-            now += 0.03
-            issue(color, off, links)
+        missing.append(
+            {
+                (color, (dz, dy, dx))
+                for color in range(3)
+                for dy in (0, 1, -1, 2)
+                for dx in (0, 1)
+                if (dz, dy, dx) != (0, 0, 0)
+            }
+        )
+    taken = {one[2] for batch in early for one in batch if one[1] == 0}
+    now, step, batches, batch = CUTS[-1] + first_us, 0, [], []
+    while step < STEPS or actions:
+        if actions and (actions[0][0] <= now or step == STEPS):
+            one = actions.pop(0)
+            if one[1] == 0:
+                taken.add(one[2])
+            now = max(now, one[0]) + 0.02
+            batch.append(one)
         elif step < STEPS and missing[step // 3] <= taken:
             batches.append(batch)
             batch = []
             step += 1
             now += step_us
         else:
-            now = heap[0][0]
-    return batches, now
-
-
-N_PLANES = 8
-STEPS = 3 * N_PLANES
-
-
-def plane_of(rank):
-    return (rank + 1) // 2 * (1 - 2 * ((rank + 1) % 2))
-
-
-BATCHES, _ = plan()
-OFFSETS = sorted({off for batch in BATCHES for _, off, _ in batch})
+            now = actions[0][0]
+    assert not batch
+    return early, batches, now
+
+
+EARLY, BATCHES, _ = plan()
+OFFSETS = sorted({one[2][1] for batch in EARLY + BATCHES for one in batch if one[1] == 0})
 
 
 def places():
@@ -204,15 +243,22 @@
     def rows_of(k):
         return pl.ds(k * CHUNK, CHUNK)
 
+    def in_start_order(c):
+        return STARTS[c // 2] * 2 + c % 2
+
     opposite = (1 - x_hi) * 2 + core
     loads[0].wait()
     firsts = {}
-    for c in range(CHUNKS):
+
+    def start_own(c):
         for way in range(2):
-            k = way * CHUNKS + c
+            k = way * CHUNKS + in_start_order(c)
             firsts[k] = go(
                 remote(xbuf.at[tp, rows_of(k)], relay.at[k], send_sem.at[k], r1.at[k], sides[way])
             )
+
+    for c in range(3):
+        start_own(c)
     own = go(remote(xbuf.at[tp], xbuf.at[tp], send_sem.at[6 * CHUNKS], r0, partner))
 
     def pass_on(k):
@@ -235,14 +281,14 @@
         ).wait_recv()
         thirds[k] = go(remote(here, here, send_sem.at[4 * CHUNKS + k], r3.at[k], partner))
 
-    def scaled(part):
+    def weighted(wide, part):
+        cols = pl.ds(pl.multiple_of(part * COLS, COLS), COLS)
+        return (wide * gain[cols].astype(F32)[None, :]).astype(BF16), cols
+
+    def whole_part(part, first):
         wide = xbuf[part].astype(F32)
         squares = jnp.sum(wide * wide, axis=1, keepdims=True)
-        cols = pl.ds(pl.multiple_of(part * COLS, COLS), COLS)
-        return squares, (wide * gain[:, cols].astype(F32)).astype(BF16), cols
-
-    def whole_part(part, first):
-        squares, rows, cols = scaled(part)
+        rows, cols = weighted(wide, part)
         product = jnp.dot(rows, wbuf[cols, :], preferred_element_type=F32)
         total[...] = product if first else total[...] + product
         return squares
@@ -273,47 +319,6 @@
             bound = bound + short_lengths[j]
         first_b[...] = first
 
-    for one in loads[1:5]:
-        one.wait()
-    squares = whole_part(tp, True)
-    for c in range(CHUNKS):
-        for way in range(2):
-            pass_on(way * CHUNKS + c)
-        if c == 0:
-            own.wait_recv()
-            squares = squares + whole_part(x_hi * 2 + 1 - core, False)
-        if c == 1:
-            facts()
-        if c >= 1:
-            for way in range(2):
-                share(way * CHUNKS + c - 1)
-    for way in range(2):
-        share(way * CHUNKS + CHUNKS - 1)
-    late = []
-    for part in (opposite, (1 - x_hi) * 2 + 1 - core):
-        if late:
-            for k in range(2 * CHUNKS):
-                thirds[k].wait_recv()
-        more, rows, cols = scaled(part)
-        squares = squares + more
-        late.append((rows, cols))
-        total[:, :KV_COLS] += jnp.dot(rows, wbuf[cols, :KV_COLS], preferred_element_type=F32)
-    factor = lax.rsqrt(squares * (1.0 / D) + norm_eps)
-
-    def turned(half, cols):
-        rows = slice(half * BLOCK, (half + 1) * BLOCK)
-        u = total[rows, cols] * factor[rows]
-        return (u * cosine[half] + pltpu.roll(u, HD // 2, 1) * sine[half]).astype(BF16)
-
-    for half in range(2):
-        rows = slice(half * BLOCK, (half + 1) * BLOCK)
-        kv[half] = turned(half, slice(0, HD)).reshape(BLOCK // THIRD, THIRD, HD)
-        kv[2 + half] = (
-            (total[rows, HD:KV_COLS] * factor[rows])
-            .astype(BF16)
-            .reshape(BLOCK // THIRD, THIRD, HD)
-        )
-
     def chunk(color, off):
         dz, dy, dx = off
         slot = seq_of(
@@ -329,30 +334,116 @@
         ).start()
 
     def take(batch):
-        for color, off, links in batch:
+        for _, sends_it, (color, off), link in batch:
             here = chunk(color, off)
-            remote(
-                here, here, seq_send.at[color], seq_recv.at[color, OFFSETS.index(off)], target["x"]
-            ).wait_recv()
-            for link in links:
+            if not sends_it:
+                remote(
+                    here, here, seq_send.at[color], seq_recv.at[color, OFFSETS.index(off)],
+                    target["x"],
+                ).wait_recv()
+            elif off == (0, 0, 0):
+                send(color, off, link, kv.at[:, color])
+            else:
                 send(color, off, link, here)
 
-    own_copy = pltpu.make_async_copy(kv, buf.at[:, seq], own_sem)
-    own_copy.start()
-    for color in range(3):
-        for link in onward(color, (0, 0, 0), "own"):
-            send(color, (0, 0, 0), link, kv.at[:, color])
-    for rows, cols in late:
-        total[:, KV_COLS:] += jnp.dot(rows, wbuf[cols, KV_COLS:], preferred_element_type=F32)
-    for head in range(GROUP):
+    def own_copy(color):
+        return pltpu.make_async_copy(kv.at[:, color], buf.at[:, seq, color], own_sem.at[color])
+
+    far_parts = (opposite, (1 - x_hi) * 2 + 1 - core)
+
+    def third(color):
+        spans = [slice(half * BLOCK + color * THIRD, half * BLOCK + (color + 1) * THIRD)
+                 for half in range(2)]
+        for k in (2 * color, 2 * color + 1):
+            for way in range(2):
+                thirds[way * CHUNKS + k].wait_recv()
+        sums = jnp.concatenate([squares[span] for span in spans])
+        product = jnp.concatenate([total[span, :KV_COLS] for span in spans])
+        kept = []
+        for part in far_parts:
+            wide = jnp.concatenate([xbuf[part, span] for span in spans]).astype(F32)
+            sums = sums + jnp.sum(wide * wide, axis=1, keepdims=True)
+            rows, cols = weighted(wide, part)
+            kept.append(rows)
+            product = product + jnp.dot(
+                rows, wbuf[cols, :KV_COLS], preferred_element_type=F32
+            )
+        factor = lax.rsqrt(sums * (1.0 / D) + norm_eps)
+        product = product * factor
+        u = product[:, :HD]
+        turned_u = pltpu.roll(u, HD // 2, 1)
         for half in range(2):
-            q[half, head * BLOCK : (head + 1) * BLOCK] = turned(
-                half, slice(KV_COLS + head * HD, KV_COLS + (head + 1) * HD)
-            )
+            rows = slice(half * THIRD, (half + 1) * THIRD)
+            angle = slice(color * THIRD, (color + 1) * THIRD)
+            kv[half, color] = (
+                u[rows] * cosine[half, angle] + turned_u[rows] * sine[half, angle]
+            ).astype(BF16)
+            kv[2 + half, color] = product[rows, HD:].astype(BF16)
+        own_copy(color).start()
+        return kept, factor
+
+    for one in loads[1:5]:
+        one.wait()
+    squares = whole_part(tp, True)
+    late = []
+    def both(do, c):
+        for way in range(2):
+            do(way * CHUNKS + in_start_order(c))
+
+    both(pass_on, 0)
+    start_own(3)
+    own.wait_recv()
+    squares = squares + whole_part(x_hi * 2 + 1 - core, False)
+    both(pass_on, 1)
+    start_own(4)
+    both(pass_on, 2)
+    start_own(5)
+    facts()
+    both(share, 0)
+    both(pass_on, 3)
+    both(share, 1)
+    both(pass_on, 4)
+    late.append(third(STARTS[0]))
+    take(EARLY[0])
+    both(share, 2)
+    both(pass_on, 5)
+    both(share, 3)
+    both(share, 4)
+    take(EARLY[1])
+    late.append(third(STARTS[1]))
+    take(EARLY[2])
+    both(share, 5)
+    take(EARLY[3])
+    late.append(third(STARTS[2]))
+    take(EARLY[4])
+    for n, part in enumerate(far_parts):
+        cols = pl.ds(pl.multiple_of(part * COLS, COLS), COLS)
+        product = jnp.dot(
+            jnp.concatenate([kept[n] for kept, _ in late]), wbuf[cols, KV_COLS:],
+            preferred_element_type=F32,
+        )
+        for at, color in enumerate(STARTS):
+            for half in range(2):
+                first = half * BLOCK + color * THIRD
+                there = (2 * at + half) * THIRD
+                total[first : first + THIRD, KV_COLS:] += product[there : there + THIRD]
+    for half in range(2):
+        factor = jnp.concatenate(
+            [late[STARTS.index(color)][1][half * THIRD : (half + 1) * THIRD] for color in range(3)]
+        )
+        for head in range(GROUP):
+            u = total[
+                half * BLOCK : (half + 1) * BLOCK,
+                KV_COLS + head * HD : KV_COLS + (head + 1) * HD,
+            ] * factor
+            q[half, head * BLOCK : (head + 1) * BLOCK] = (
+                u * cosine[half] + pltpu.roll(u, HD // 2, 1) * sine[half]
+            ).astype(BF16)
     m_ref[...] = jnp.full(m_ref.shape, NEG, F32)
     l_ref[...] = jnp.zeros(l_ref.shape, F32)
     acc_ref[...] = jnp.zeros(acc_ref.shape, F32)
-    own_copy.wait()
+    for color in range(3):
+        own_copy(color).wait()
 
     def step(half, region, plane, allowed):
         slots = pl.ds(plane * SLOTS, SLOTS)
@@ -412,25 +503,86 @@
             if batch:
                 pl.when(unit == k)(functools.partial(take, batch))
 
+    def finish(half):
+        ready = jnp.transpose(acc_ref[half] / l_ref[half]).astype(BF16)
+        for head in range(GROUP):
+            attended[half * BLOCK : (half + 1) * BLOCK, head * HD : (head + 1) * HD] = ready[
+                head * BLOCK : (head + 1) * BLOCK
+            ]
+
+    far = (1 - x_hi) * 2
+    near = x_hi * 2
+
+    def terms(part, half):
+        cols = pl.ds(pl.multiple_of(part * COLS, COLS), COLS)
+        return jnp.dot(
+            attended[half * BLOCK : (half + 1) * BLOCK, :], wout[:, cols],
+            preferred_element_type=F32,
+        )
+
+    def partner_copy(which, half):
+        rows = pl.ds(half * BLOCK, BLOCK)
+        k = 2 * which + half
+        return remote(
+            sendp.at[which, rows], recvp.at[which, rows], out_send.at[4 * CHUNKS + k], rp.at[k],
+            partner,
+        )
+
+    def to_partner(which, half, part):
+        sendp[which, pl.ds(half * BLOCK, BLOCK)] = terms(part, half).astype(BF16)
+        partner_copy(which, half).start()
+
+    def hop(k):
+        return remote(
+            sendx.at[rows_of(k)], relay_out.at[k], out_send.at[k], o1.at[k], sides[k % 2]
+        )
+
+    def land(k):
+        return remote(
+            relay_out.at[k], recvx.at[rows_of(k)], out_send.at[2 * CHUNKS + k], o2.at[k],
+            sides[k % 2],
+        )
+
+    def chunks_of(half):
+        return range(half * CHUNKS, (half + 1) * CHUNKS)
+
+    def cross(half, mine):
+        rows = pl.ds(half * BLOCK, BLOCK)
+        partner_copy(0, half).wait_recv()
+        sendx[rows] = (mine + recvp[0, rows].astype(F32)).astype(BF16)
+        for k in chunks_of(half):
+            hop(k).start()
+
+    loads[5].wait()
+
     @pl.loop(0, N_PLANES)
     def _(unit):
         dz = (unit + 1) // 2 * (1 - 2 * ((unit + 1) % 2))
         plane = (z + dz + 8) % 8
         batch_at(unit, 0)
 
+        @pl.when(plane < z)
+        def _():
+            step(0, 0, plane, None)
+
+        @pl.when(plane == z)
+        def _():
+            masked_a(plane)
+
+        @pl.when(unit == N_PLANES - 1)
+        def _():
+            finish(0)
+            to_partner(0, 0, far + 1 - core)
+
+        batch_at(unit, 1)
+
         @pl.when(in_long == 1)
         def _():
             step(1, 0, plane, None)
 
-        batch_at(unit, 1)
-
-        @pl.when(plane < z)
+        @pl.when(unit == N_PLANES - 1)
         def _():
-            step(0, 0, plane, None)
-
-        @pl.when(plane == z)
-        def _():
-            masked_a(plane)
+            cross(0, terms(far + core, 0))
 
         batch_at(unit, 2)
 
@@ -442,57 +594,15 @@
         def _():
             masked_b(plane)
 
+    finish(1)
+    to_partner(0, 1, far + 1 - core)
+    mine = terms(far + core, 1)
     for half in range(2):
-        ready = jnp.transpose(acc_ref[half] / l_ref[half]).astype(BF16)
-        for head in range(GROUP):
-            attended[half * BLOCK : (half + 1) * BLOCK, head * HD : (head + 1) * HD] = ready[
-                head * BLOCK : (head + 1) * BLOCK
-            ]
-
-    loads[5].wait()
-    far = (1 - x_hi) * 2
-    near = x_hi * 2
-
-    def terms(part, way):
-        cols = pl.ds(pl.multiple_of(part * COLS, COLS), COLS)
-        rows = slice(way * BLOCK, (way + 1) * BLOCK)
-        return jnp.dot(attended[rows, :], wout[:, cols], preferred_element_type=F32)
-
-    def to_partner(which, way, part):
-        rows = pl.ds(way * BLOCK, BLOCK)
-        sendp[which, rows] = terms(part, way).astype(BF16)
-        k = 2 * which + way
-        return go(
-            remote(
-                sendp.at[which, rows], recvp.at[which, rows], out_send.at[4 * CHUNKS + k],
-                rp.at[k], partner,
-            )
-        )
-
-    far_copies = [to_partner(0, way, far + 1 - core) for way in range(2)]
-    hops = {}
-    for way in range(2):
-        rows = pl.ds(way * BLOCK, BLOCK)
-        mine = terms(far + core, way)
-        far_copies[way].wait_recv()
-        sendx[rows] = (mine + recvp[0, rows].astype(F32)).astype(BF16)
-        for c in range(CHUNKS):
-            k = way * CHUNKS + c
-            hops[k] = go(
-                remote(sendx.at[rows_of(k)], relay_out.at[k], out_send.at[k], o1.at[k], sides[way])
-            )
-    near_copies = [to_partner(1, way, near + 1 - core) for way in range(2)]
-    lands = {}
-    for c in range(CHUNKS):
-        for way in range(2):
-            k = way * CHUNKS + c
-            hops[k].wait_recv()
-            lands[k] = go(
-                remote(
-                    relay_out.at[k], recvx.at[rows_of(k)], out_send.at[2 * CHUNKS + k], o2.at[k],
-                    sides[way],
-                )
-            )
+        to_partner(1, half, near + 1 - core)
+    cross(1, mine)
+    for k in chunks_of(0):
+        hop(k).wait_recv()
+        land(k).start()
     for page in range(ROWS // PAGE):
         ids = lax.broadcasted_iota(jnp.int32, page_slot.shape, 0) * page_slot.shape[
             1
@@ -504,17 +614,26 @@
         slot = block + region * (LAST_BLOCK - 2 * block)
         pages[page, 0] = buf[region, slot, part]
         pages[page, 1] = buf[region + 2, slot, part]
+    for k in chunks_of(1):
+        hop(k).wait_recv()
+        land(k).start()
     own_x = xbuf[tp].astype(F32)
-    for way in range(2):
-        rows = slice(way * BLOCK, (way + 1) * BLOCK)
-        kept = terms(near + core, way) + own_x[rows]
-        near_copies[way].wait_recv()
+    for half in range(2):
+        rows = slice(half * BLOCK, (half + 1) * BLOCK)
+        kept = terms(near + core, half) + own_x[rows]
+        partner_copy(1, half).wait_recv()
         kept = kept + recvp[1, rows].astype(F32)
-        for c in range(CHUNKS):
-            lands[way * CHUNKS + c].wait_recv()
+        for k in chunks_of(half):
+            land(k).wait_recv()
         out[rows, :] = (kept + recvx[rows].astype(F32)).astype(BF16)
     for one in sends:
         one.wait_send()
+    for half in range(2):
+        for which in range(2):
+            partner_copy(which, half).wait_send()
+        for k in chunks_of(half):
+            hop(k).wait_send()
+            land(k).wait_send()
     for color in range(3):
         sent = buf.at[:, pl.ds(0, N_SEQ - 1), color]
         pltpu.make_async_copy(sent, sent, seq_send.at[color]).wait()
@@ -524,6 +643,10 @@
 SM = pl.BlockSpec(memory_space=pltpu.SMEM)
 ANY = pl.BlockSpec(memory_space=pl.ANY)
 DMA = pltpu.SemaphoreType.DMA
+
+
+def in_hbm(one):
+    return pltpu.with_memory_space_constraint(one, pltpu.HBM)
 
 
 def local(hidden_in, norm_gain, w_query, w_key, w_value, w_out, short_lengths, page_slot):
@@ -566,7 +689,7 @@
             DMA((2 * CHUNKS,)),
             DMA((2 * CHUNKS,)),
             DMA((2 * CHUNKS,)),
-            DMA(()),
+            DMA((3,)),
             DMA((3,)),
             DMA((3, len(OFFSETS))),
             DMA((4 * CHUNKS + 4,)),
@@ -575,20 +698,20 @@
             DMA((2 * CHUNKS,)),
         ],
         compiler_params=pltpu.CompilerParams(
-            collective_id=0, has_side_effects=True, vmem_limit_bytes=60 * 1024 * 1024
+            collective_id=0, has_side_effects=True, vmem_limit_bytes=44 * 1024 * 1024
         ),
         name="layer",
-    )(
+    )(*(in_hbm(one) for one in (
         short_lengths,
         hidden_in,
-        norm_gain.reshape(1, D),
+        norm_gain,
         jnp.asarray(frequency),
         page_slot.reshape(-1, HD),
         w_query,
         w_key,
         w_value,
         w_out,
-    )
+    )))
 
 
 def solution(mesh):

time: 127 us -> 118 us (0.929)
  Pallas kernels: 121 us -> 116 us
  local copies, waits for them, and re-layouts: 4.83 us -> 1.49 us
    pallas_call x1, Pallas kernels: 121 us -> 116 us  [local(): pl.pallas_call(layer_kernel, out_shape=(jax.ShapeDtypeStruct((ROWS, COLS)...]
    unnamed x2, local copies, waits for them, and re-layouts: 3.53 us -> 1.49 us
    reshape x1 -> x0, local copies, waits for them, and re-layouts: 1.3 us -> none  [local(): norm_gain.reshape(1, D)]
where the time goes in v4:
time: 118 us
  Pallas kernels  116 us (98%)
  local copies, waits for them, and re-layouts  1.49 us (1%)
    pallas_call x1, Pallas kernels, local(): pl.pallas_call(layer_kernel, out_shape=(jax.ShapeDtypeStruct((ROWS, COLS)...  116 us

profile of v4, /device:TPU:193, one launch (start us, length us, event | category | flops | bytes accessed | tf_op | source)
XLA Modules:
  0.0 118.3 jit_solution(10849298193352096540)
XLA Ops:
  0.6 116.1 %layer.1 = (bf16[384,768]{1,0:T(8,128)(2,1)S(1)}, bf16[6,2,64,128]{3,2,1,0:T(8,128)(2,1)S(1)}) custom-call(s32[14]{0:T(128)} %short_lengths.1, bf16[384,768]{1,0:T(8,128)(2,1)} %hidden.1, bf16[3072]{0:T(1024)(128)(2,1)} %gain.1, f32[1,128]{1,0:T(1,128)} %constant.2.clone.frequency, s32[3,128]{1,0:T(4,128)} %bitcast.1, bf16[3072,384]{1,0:T(8,128)(2,1)} %wq.1, ...), custom_call_target="tpu_custom_call" | custom-call | tf_op jit(solution)/shard_map/layer/pallas_call | solution.py:656
  116.8 0.8 copy.13
  117.6 0.7 copy.14

commit v5 on v4

--- a/solution.py
+++ b/solution.py
@@ -76,7 +76,7 @@
     return (rank + 1) // 2 * (1 - 2 * ((rank + 1) % 2))
 
 
-def timetable(copy_us=1.41, hop_us=1.7, ahead_us=4.0):
+def timetable(copy_us=1.65, hop_us=1.8, ahead_us=8.0):
     heap, count, queues, busy, arrived, served = [], 0, {}, {}, {}, []
 
     def put(now, what):
@@ -116,7 +116,7 @@
     return actions
 
 
-def plan(step_us=1.2, first_us=1.5):
+def plan(step_us=1.7, first_us=1.5):
     actions = timetable()
     early = []
     for cut in CUTS:
@@ -319,12 +319,14 @@
             bound = bound + short_lengths[j]
         first_b[...] = first
 
+    at_z = {dz: lax.rem(z + (dz + 8), 8) * 8 for dz in range(-3, 5)}
+    at_y = {dy: lax.rem(y + (dy + 4), 4) * 2 for dy in range(-1, 3)}
+    at_x = (x_lo, 1 - x_lo)
+    at_yx = {(dy, dx): at_y[dy] + at_x[dx] for dy in at_y for dx in range(2)}
+
     def chunk(color, off):
         dz, dy, dx = off
-        slot = seq_of(
-            lax.rem(z + (dz + 8), 8), lax.rem(y + (dy + 4), 4), x_lo if dx == 0 else 1 - x_lo
-        )
-        return buf.at[:, slot, color]
+        return buf.at[:, at_z[dz] + at_yx[dy, dx], color]
 
     def send(color, off, link, src):
         there = shifted(off, link)

time: 118 us -> 113 us (0.958)
  Pallas kernels: 116 us -> 111 us
    pallas_call x1, Pallas kernels: 116 us -> 111 us  [local(): pl.pallas_call(layer_kernel, out_shape=(jax.ShapeDtypeStruct((ROWS, COLS)...]
where the time goes in v5:
time: 113 us
  Pallas kernels  111 us (98%)
  local copies, waits for them, and re-layouts  1.49 us (1%)
    pallas_call x1, Pallas kernels, local(): pl.pallas_call(layer_kernel, out_shape=(jax.ShapeDtypeStruct((ROWS, COLS)...  111 us

profile of v5, /device:TPU:193, one launch (start us, length us, event | category | flops | bytes accessed | tf_op | source)
XLA Modules:
  0.0 113.1 jit_solution(11788731163223633849)
XLA Ops:
  0.6 111.0 %layer.1 = (bf16[384,768]{1,0:T(8,128)(2,1)S(1)}, bf16[6,2,64,128]{3,2,1,0:T(8,128)(2,1)S(1)}) custom-call(s32[14]{0:T(128)} %short_lengths.1, bf16[384,768]{1,0:T(8,128)(2,1)} %hidden.1, bf16[3072]{0:T(1024)(128)(2,1)} %gain.1, f32[1,128]{1,0:T(1,128)} %constant.2.clone.frequency, s32[3,128]{1,0:T(4,128)} %bitcast.1, bf16[3072,384]{1,0:T(8,128)(2,1)} %wq.1, ...), custom_call_target="tpu_custom_call" | custom-call | tf_op jit(solution)/shard_map/layer/pallas_call | solution.py:658
  111.7 0.8 copy.13
  112.5 0.7 copy.14

commit v6 on v5

--- a/solution.py
+++ b/solution.py
@@ -76,7 +76,7 @@
     return (rank + 1) // 2 * (1 - 2 * ((rank + 1) % 2))
 
 
-def timetable(copy_us=1.65, hop_us=1.8, ahead_us=8.0):
+def timetable(copy_us=1.65, hop_us=1.9, ahead_us=8.0):
     heap, count, queues, busy, arrived, served = [], 0, {}, {}, {}, []
 
     def put(now, what):
@@ -116,7 +116,7 @@
     return actions
 
 
-def plan(step_us=1.7, first_us=1.5):
+def plan(step_us=1.6, first_us=1.5):
     actions = timetable()
     early = []
     for cut in CUTS:

time: 113 us -> 113 us (level)
  no operation moved by 1% of the time
where the time goes in v6:
time: 113 us
  Pallas kernels  111 us (98%)
  local copies, waits for them, and re-layouts  1.49 us (1%)
    pallas_call x1, Pallas kernels, local(): pl.pallas_call(layer_kernel, out_shape=(jax.ShapeDtypeStruct((ROWS, COLS)...  111 us

profile of v6, /device:TPU:193, one launch (start us, length us, event | category | flops | bytes accessed | tf_op | source)
XLA Modules:
  0.0 113.1 jit_solution(13817371965844325348)
XLA Ops:
  0.6 111.0 %layer.1 = (bf16[384,768]{1,0:T(8,128)(2,1)S(1)}, bf16[6,2,64,128]{3,2,1,0:T(8,128)(2,1)S(1)}) custom-call(s32[14]{0:T(128)} %short_lengths.1, bf16[384,768]{1,0:T(8,128)(2,1)} %hidden.1, bf16[3072]{0:T(1024)(128)(2,1)} %gain.1, f32[1,128]{1,0:T(1,128)} %constant.2.clone.frequency, s32[3,128]{1,0:T(4,128)} %bitcast.1, bf16[3072,384]{1,0:T(8,128)(2,1)} %wq.1, ...), custom_call_target="tpu_custom_call" | custom-call | tf_op jit(solution)/shard_map/layer/pallas_call | solution.py:658
  111.6 0.8 copy.13
  112.4 0.7 copy.14
